TPU v7x, 512 devices: a whole 4x8x8 slice. The times are simulated.
512 devices in a mesh: dp: 16 (over z, x_lo), space: 32 (over y, x_hi, core).
Axes of the slice: x: 4 (x_hi: 2, x_lo: 2; x = x_hi * 2 + x_lo), y: 8, z: 8, core: 2. Of those that a mesh axis runs over, the one named last changes fastest.
Arguments:
- features: bfloat16 [16, 64, 72, 2048], P('dp', 'space'), may hold values from -150 to 150
- depthwise: bfloat16 [2, 9, 2048], replicated, may hold values from -2 to 2
- pointwise: bfloat16 [2048, 512], replicated, may hold values from -0.125 to 0.125
- bn_gain: float32 [2, 2048], replicated, may hold values from 0.1 to 1.9
- cotangent: bfloat16 [16, 64, 72, 256], P('dp', 'space'), may hold values from -6 to 6
Outputs:
- block_out: bfloat16 [16, 64, 72, 256], P('dp', 'space')
- grad_pointwise: float32 [2048, 512], P('space')
- grad_depthwise: float32 [2, 9, 2048], P(None, None, 'space')
All inputs are finite; a program needn't handle non-finite values.
Results may differ from a plain program's by a relative error of at most 0.001.
The roundings to bfloat16 on the way count: a program that leaves them out, or rounds other values in their place, can miss the bound.
Values may be sent and summed in bfloat16 or wider, within the bound.
No kernel may reach another device: no remote copies, remote signals or barrier semaphores. Data moves between devices by JAX's collectives and lax.ppermute only.
A program may use at most 64 MiB of HBM per device.

v0:
```python
import functools

import jax
import jax.numpy as jnp
from jax import lax
from jax.experimental import pallas as pl
from jax.experimental.pallas import tpu as pltpu
from jax.sharding import Mesh, PartitionSpec as P

NEAR_DILATION = 12
FAR_DILATION = 24
DILATIONS = (NEAR_DILATION, FAR_DILATION)
eps_norm = 1e-05

GROUP = ("y", "xh")
ORDER = ((-1,), (0,), (1,), (-3, -2), (2, 3), (-4,))
DP = ("z", "xl")
ROWS = ("z", "xl", "core")
f32 = jnp.float32
bf16 = jnp.bfloat16


def exchange(value, axes):
    return lax.all_to_all(value, axes, 0, 0, tiled=True)


def shifted(value, steps):
    count = lax.axis_size("y")
    return lax.ppermute(value, "y", [(i, (i + steps) % count) for i in range(count)])


def call(kernel, outs, *args, scratch=(), smem=(), slow=()):
    vmem = pl.BlockSpec(memory_space=pltpu.VMEM)
    specs = [pl.BlockSpec(memory_space=pltpu.SMEM) if i in smem else vmem for i in range(len(args))]
    args = [
        pltpu.with_memory_space_constraint(a, pltpu.HBM) if i in slow else a for i, a in enumerate(args)
    ]
    return pl.pallas_call(
        kernel,
        out_shape=[pltpu.HBM(*o[:2]) if len(o) == 3 else jax.ShapeDtypeStruct(*o) for o in outs],
        in_specs=specs,
        out_specs=[vmem] * len(outs),
        scratch_shapes=list(scratch),
        compiler_params=pltpu.CompilerParams(vmem_limit_bytes=24 << 20),
    )(*args)


def pack_kernel(feat_ref, out_ref):
    groups, _, block = out_ref.shape
    for g in range(groups):
        out_ref[g] = feat_ref[:, g * block : (g + 1) * block]


def fill_padded(held_ref, pad):
    groups = held_ref.shape[0]
    total, rows, wide, block = pad.shape
    lead = (total - groups) // 2
    width = held_ref.shape[1] // rows
    edge = (wide - width) // 2
    for i in range(lead):
        pad[i] = jnp.zeros((rows, wide, block), f32)
        pad[lead + groups + i] = jnp.zeros((rows, wide, block), f32)

    def step(g, carry):
        value = held_ref[g].astype(f32).reshape(rows, width, block)
        pad[lead + g, :, :edge, :] = jnp.zeros((rows, edge, block), f32)
        pad[lead + g, :, edge + width :, :] = jnp.zeros((rows, edge, block), f32)
        pad[lead + g, :, edge : edge + width, :] = value
        return carry

    lax.fori_loop(0, groups, step, 0)


def tap(pad, g, k, a, b, row_step, width, groups):
    lead = (pad.shape[0] - groups) // 2
    edge = (pad.shape[2] - width) // 2
    row = g + lead + (a - 1) * DILATIONS[k] // row_step
    col = edge + (b - 1) * DILATIONS[k]
    return pad[row, :, col : col + width, :]


def fold(value):
    lanes = value.shape[-1]
    return jnp.sum(value.reshape(-1, 8, lanes), axis=0)


def forward_kernel(row_step, held_ref, taps_ref, z_ref, sums_ref, pad):
    groups, pixels = held_ref.shape[:2]
    rows, block = pad.shape[1], pad.shape[3]
    width = pixels // rows
    fill_padded(held_ref, pad)

    def step(g, carry):
        carry = list(carry)
        for k in range(2):
            total = jnp.zeros((rows, width, block), f32)
            for a in range(3):
                for b in range(3):
                    t = 9 * k + 3 * a + b
                    total = total + taps_ref[t : t + 1, :][None] * tap(pad, g, k, a, b, row_step, width, groups)
            value = total.reshape(pixels, block).astype(bf16)
            z_ref[k, g] = value
            value = value.astype(f32)
            carry[2 * k] = carry[2 * k] + fold(value)
            carry[2 * k + 1] = carry[2 * k + 1] + fold(value * value)
        return tuple(carry)

    zero = jnp.zeros((8, block), f32)
    sums = lax.fori_loop(0, groups, step, (zero,) * 4)
    sums = [jnp.sum(s, axis=0, keepdims=True) for s in sums]
    line = lax.broadcasted_iota(jnp.int32, (8, block), 0)
    tile = zero
    for i, s in enumerate(sums):
        tile = jnp.where(line == i, s, tile)
    for i in range(sums_ref.shape[0]):
        sums_ref[i] = tile


def norm_kernel(count, z_ref, sums_ref, gain_ref, used_ref, params_ref):
    groups, block = z_ref.shape[1], z_ref.shape[3]
    sums = jnp.sum(sums_ref[...], axis=0)
    line = lax.broadcasted_iota(jnp.int32, (8, block), 0)
    tile = jnp.zeros((8, block), f32)
    stats = []
    for k in range(2):
        average = sums[2 * k : 2 * k + 1] / count
        variance = sums[2 * k + 1 : 2 * k + 2] / count - average * average
        inv = lax.rsqrt(variance + eps_norm)
        tile = jnp.where(line == 2 * k, average, tile)
        tile = jnp.where(line == 2 * k + 1, inv, tile)
        stats.append((average, inv))
    params_ref[...] = tile

    def step(g, carry):
        for k in range(2):
            average, inv = stats[k]
            xhat = (z_ref[k, g].astype(f32) - average) * inv
            scaled = gain_ref[k : k + 1, :] * xhat
            used_ref[g, :, k * block : (k + 1) * block] = jnp.maximum(scaled, 0.0).astype(bf16)
        return carry

    lax.fori_loop(0, groups, step, 0)


def place_of(i):
    return i % 2, i // 2 % 2, i // 4


def back_kernel(place_ref, z_ref, params_ref, gain_ref, *refs):
    *pair_refs, maps_ref, dxhat_ref, keep_ref, send_ref, total_ref, cots_ref = refs
    _, groups, _, block = z_ref.shape
    params = params_ref[...]
    gain = gain_ref[...]
    rows, half = groups // 2, place_ref[1]
    zero = jnp.zeros((8, block), f32)
    total_ref[...] = jnp.zeros_like(total_ref)
    for aparts, ref in zip(ORDER, pair_refs, strict=True):
        for i, apart in enumerate(aparts):
            row = (place_ref[0] + apart + rows) % rows
            for slot in range(2):
                cots_ref[2 * row + (half ^ slot)] = ref[2 * i + slot]

    def step(g, carry):
        carry = list(carry)
        cot = cots_ref[g]
        back = jnp.dot(cot, maps_ref[...], preferred_element_type=f32)
        used = []
        for k in range(2):
            xhat = (z_ref[k, g].astype(f32) - params[2 * k : 2 * k + 1]) * params[2 * k + 1 : 2 * k + 2]
            scaled = gain[k : k + 1] * xhat
            used.append(jnp.maximum(scaled, 0.0).astype(bf16))
            dxhat = jnp.where(scaled > 0, back[:, k * block : (k + 1) * block], 0.0) * gain[k : k + 1]
            dxhat_ref[k, g] = dxhat
            carry[2 * k] = carry[2 * k] + fold(dxhat)
            carry[2 * k + 1] = carry[2 * k + 1] + fold(dxhat * xhat)
        for k in range(2):
            total_ref[k * block : (k + 1) * block, :] += lax.dot_general(
                used[k], cot, (((0,), (0,)), ((), ())), preferred_element_type=f32
            )
        return tuple(carry)

    sums = lax.fori_loop(0, groups, step, (zero,) * 4)
    line = lax.broadcasted_iota(jnp.int32, (8, block), 0)
    tile = zero
    for i, s in enumerate(sums):
        tile = jnp.where(line == i, jnp.sum(s, axis=0, keepdims=True), tile)
    core = place_ref[2]
    for ref, k in ((keep_ref, core), (send_ref, 1 - core)):
        ref[:block, :] = total_ref[pl.ds(pl.multiple_of(k * block, block), block), :]
        ref[block:, :block] = tile
        ref[block:, block:] = tile


def filter_kernel(row_step, count, held_ref, z_ref, params_ref, dxhat_ref, got_ref, out_ref, pad):
    groups, pixels = held_ref.shape[:2]
    rows, block = pad.shape[1], pad.shape[3]
    width = pixels // rows
    share = block // 2
    fill_padded(held_ref, pad)
    got = jnp.sum(got_ref[...], axis=0)
    lines = (got.shape[0] - 8) // 2
    seconds = got[2 * lines :] / count
    params = params_ref[...]
    zero = jnp.zeros((8, block), f32)
    grads = []
    for k in range(2):

        def step(g, carry, k=k):
            carry = list(carry)
            xhat = (z_ref[k, g].astype(f32) - params[2 * k : 2 * k + 1]) * params[2 * k + 1 : 2 * k + 2]
            inner = dxhat_ref[k, g] - seconds[2 * k : 2 * k + 1] - xhat * seconds[2 * k + 1 : 2 * k + 2]
            dz = (params[2 * k + 1 : 2 * k + 2] * inner).astype(bf16).astype(f32).reshape(rows, width, block)
            for a in range(3):
                for b in range(3):
                    moved = tap(pad, g, k, a, b, row_step, width, groups)
                    carry[3 * a + b] = carry[3 * a + b] + fold(dz * moved)
            return tuple(carry)

        grads.append([jnp.sum(s, axis=0, keepdims=True) for s in lax.fori_loop(0, groups, step, (zero,) * 9)])
    line = lax.broadcasted_iota(jnp.int32, (16, block), 0)
    tiles = []
    for k in range(2):
        tile = jnp.zeros((16, block), f32)
        for t in range(9):
            tile = jnp.where(line == t, grads[k][t], tile)
        tiles.append(tile)
    low = lax.broadcasted_iota(jnp.int32, (16, block), 1) < share
    halves = (
        jnp.where(low, tiles[0], pltpu.roll(tiles[1], share, 1)),
        jnp.where(low, pltpu.roll(tiles[0], share, 1), tiles[1]),
    )
    for i in range(out_ref.shape[0]):
        out_ref[i, :lines, :] = got[i % 2 * lines : (i % 2 + 1) * lines]
        out_ref[i, lines:, :] = halves[i % 2]


def mix_kernel(whole_ref, maps_ref, out_ref):
    groups, pixels, both = whole_ref.shape
    block = both // 2
    outs = out_ref.shape[1]
    total = jnp.zeros((pixels, outs), f32)
    for g in range(groups):
        for k in range(2):
            total = total + jnp.dot(
                whole_ref[g, :, k * block : (k + 1) * block],
                maps_ref[g * block : (g + 1) * block, k * outs : (k + 1) * outs],
                preferred_element_type=f32,
            )
    out_ref[...] = total.astype(bf16)


def last_kernel(got_ref, pw_ref, dw_ref):
    peers, total, block = got_ref.shape
    share, wide = pw_ref.shape
    lines = total - 16
    lanes = wide // 2 // block
    for i in range(peers):
        k, lane, row = place_of(i)
        left = (k * lanes + lane) * block
        pw_ref[row * lines : (row + 1) * lines, left : left + block] = got_ref[i, :lines, :]
    dw = jnp.sum(got_ref[:, lines:, :], axis=0)
    dw_ref[:, 0, :] = dw[:9, :share]
    dw_ref[:, 1, :] = pltpu.roll(dw, share, 1)[:9, :share]


def body(features, depthwise, pointwise, bn_gain, cotangent):
    _, row_count, width, channels = features.shape
    outs = cotangent.shape[3]
    groups = lax.axis_size(GROUP)
    peers = lax.axis_size(ROWS)
    samples = lax.axis_size(DP)
    cores = lax.axis_size("core")
    block = channels // groups
    share = block // cores
    pixels = row_count * width
    row_step = row_count * cores
    count = float(samples * groups * cores * pixels)
    mine = lax.axis_index(GROUP)
    lead = FAR_DILATION // row_step
    pad = pltpu.VMEM((groups + 2 * lead, row_count, width + 2 * FAR_DILATION, block), f32)
    lines = share * 2 * outs // peers // block

    (sent,) = call(pack_kernel, [((groups, pixels, block), bf16, None)], features.reshape(pixels, channels), slow=(0,))
    held = exchange(sent, GROUP)
    cot = cotangent.reshape(1, pixels, outs)
    pairs = [jnp.concatenate([cot, lax.ppermute(cot, "xh", [(0, 1), (1, 0)])], axis=0)]
    pair = pairs[0]
    above, below = shifted(pair, 1), shifted(pair, -1)
    left, right = jnp.concatenate([above, pair], axis=0), jnp.concatenate([pair, below], axis=0)
    taps = lax.dynamic_slice_in_dim(depthwise, mine * block, block, 2).astype(f32).reshape(18, block)
    held, left, right, taps = lax.optimization_barrier((held, left, right, taps))
    gain = lax.dynamic_slice_in_dim(bn_gain, mine * block, block, 1)
    maps = lax.dynamic_slice_in_dim(pointwise, mine * block, block, 0)
    maps = maps.reshape(block, 2, outs).transpose(2, 1, 0).reshape(outs, 2 * block)

    z, sums = call(
        functools.partial(forward_kernel, row_step),
        [((2, groups, pixels, block), bf16), ((peers, 8, block), f32, None)],
        held,
        taps,
        scratch=[pad],
    )
    sums, left, right = lax.optimization_barrier((sums, left, right))
    sums = exchange(sums, ROWS)
    left = shifted(left, 2)
    right = shifted(right, -2)
    pairs = [above, pair, below, left, right, shifted(left[:2], 1)]
    used, params = call(
        functools.partial(norm_kernel, count),
        [((groups, pixels, 2 * block), bf16, None), ((8, block), f32)],
        z,
        sums,
        gain,
    )
    whole = exchange(used, GROUP)
    dxhat, keep, sent = call(
        back_kernel,
        [((2, groups, pixels, block), f32, None)] + [((block + 8, outs), f32)] * 2,
        jnp.stack([lax.axis_index("y"), lax.axis_index("xh"), lax.axis_index("core")]).astype(jnp.int32),
        z,
        params,
        gain,
        *pairs,
        maps,
        slow=range(4, 4 + len(pairs)),
        scratch=[pltpu.VMEM((2 * block, outs), f32), pltpu.VMEM((groups, pixels, outs), bf16)],
        smem=(0,),
    )
    keep = keep + lax.ppermute(sent, "core", [(0, 1), (1, 0)])
    side = lax.axis_index("xl")
    sent = lax.dynamic_slice_in_dim(keep, (1 - side) * block, block, 1)
    keep = lax.dynamic_slice_in_dim(keep, side * block, block, 1)
    keep = keep + lax.ppermute(sent, "xl", [(0, 1), (1, 0)])
    layers = lax.axis_size("z")
    sent = keep[:block].reshape(cores, layers, lines, block).transpose(1, 0, 2, 3).reshape(layers, cores * lines, block)
    sent = jnp.concatenate([sent, jnp.broadcast_to(keep[block:], (layers, 8, block))], axis=1)
    whole, sent = lax.optimization_barrier((whole, sent))
    got = exchange(sent, "z")
    (sent,) = call(
        functools.partial(filter_kernel, row_step, count),
        [((peers, lines + 16, block), f32, None)],
        held,
        z,
        params,
        dxhat,
        got,
        slow=(3,),
        scratch=[pad],
    )
    got = exchange(sent, ROWS)
    (block_out,) = call(mix_kernel, [((pixels, outs), bf16, None)], whole, pointwise, slow=(1,))
    grad_pw, grad_dw = call(last_kernel, [((share, 2 * outs), f32, None), ((9, 2, share), f32, None)], got)
    return block_out.reshape(1, row_count, width, outs), grad_pw, grad_dw.transpose(1, 0, 2)


def solution(mesh):
    fine = Mesh(mesh.devices.reshape(8, 2, 8, 2, 2), ("z", "xl", "y", "xh", "core"))
    space = ("y", "xh", "core")
    in_specs = (P(DP, space, None, None), P(), P(), P(), P(DP, space, None, None))
    out_specs = (P(DP, space, None, None), P(space, None), P(None, None, space))
    return jax.shard_map(body, mesh=fine, in_specs=in_specs, out_specs=out_specs, check_vma=False)
```

profile of v0, /device:TPU:6, one launch (start us, length us, event | category | flops | bytes accessed | tf_op | source)
XLA Modules:
  0.0 170.6 jit_solution(7642330786537144838)
XLA Ops:
  0.7 2.1 %shard_map.76 = bf16[16,144,128]{2,1,0:T(8,128)(2,1)} custom-call(bf16[144,2048]{1,0:T(8,128)(2,1)} %bitcast.21), custom_call_target="tpu_custom_call" | custom-call | tf_op jit(solution)/shard_map/pallas_call | solution.py:38
  2.7 10.1 %all-to-all-start = ((bf16[16,144,128]{2,1,0:T(8,128)(2,1)}), bf16[16,144,128]{2,1,0:T(8,128)(2,1)S(1)}, u32[]{:S(2)}, u32[]{:S(2)}) async-start(bf16[16,144,128]{2,1,0:T(8,128)(2,1)} %shard_map.76), calls=%async_computation | async-start | bytes 1179648 | tf_op jit(solution)/shard_map/all_to_all | solution.py:24
  12.8 2.0 %collective-permute-start = (bf16[1,144,256]{2,1,0:T(8,128)(2,1)S(1)}, bf16[1,144,256]{2,1,0:T(8,128)(2,1)S(1)}, u32[]{:S(2)}, u32[]{:S(2)}) collective-permute-start(bf16[1,144,256]{2,1,0:T(8,128)(2,1)S(1)} %bitcast.23), channel_id=1, source_target_pairs={{0,2},{2,0},{1,3},{3,1},{4,6},{6,4},{5,7},{7,5},{8,10},{10,8},{9,1... | collective-permute-start | bytes 221192 | tf_op jit(solution)/shard_map/ppermute | solution.py:286
  14.8 5.9 %collective-permute-done = bf16[1,144,256]{2,1,0:T(8,128)(2,1)S(1)} collective-permute-done((bf16[1,144,256]{2,1,0:T(8,128)(2,1)S(1)}, bf16[1,144,256]{2,1,0:T(8,128)(2,1)S(1)}, u32[]{:S(2)}, u32[]{:S(2)}) %collective-permute-start) | collective-permute-done | bytes 73760 | tf_op jit(solution)/shard_map/ppermute | solution.py:286
  20.7 4.6 %collective-permute-start.2 = (bf16[2,144,256]{2,1,0:T(8,128)(2,1)S(1)}, bf16[2,144,256]{2,1,0:T(8,128)(2,1)S(1)}, u32[]{:S(2)}, u32[]{:S(2)}) collective-permute-start(bf16[2,144,256]{2,1,0:T(8,128)(2,1)S(1)} %pad_maximum_fusion.2.refs_1_), channel_id=1, source_target_pairs={{0,28},{4,0},{8,4},{12,8},{16,12},{20,16},{24,20},{28,24},{1,29},{... | collective-permute-start | bytes 442376 | tf_op jit(solution)/shard_map/ppermute | solution.py:29
  28.0 2.4 %collective-permute-done.2.refs_2_ = bf16[2,144,256]{2,1,0:T(8,128)(2,1)S(1)} collective-permute-done((bf16[2,144,256]{2,1,0:T(8,128)(2,1)S(1)}, bf16[2,144,256]{2,1,0:T(8,128)(2,1)S(1)}, u32[]{:S(2)}, u32[]{:S(2)}) %collective-permute-start.2) | collective-permute-done | bytes 147488 | tf_op jit(solution)/shard_map/ppermute | solution.py:29
  30.4 3.2 %collective-permute-done.1.refs_0_ = bf16[2,144,256]{2,1,0:T(8,128)(2,1)S(1)} collective-permute-done((bf16[2,144,256]{2,1,0:T(8,128)(2,1)S(1)}, bf16[2,144,256]{2,1,0:T(8,128)(2,1)S(1)}, u32[]{:S(2)}, u32[]{:S(2)}) %collective-permute-start.1) | collective-permute-done | bytes 147488 | tf_op jit(solution)/shard_map/ppermute | solution.py:29
  34.5 2.7 %shard_map.77 = (bf16[2,16,144,128]{3,2,1,0:T(8,128)(2,1)S(1)}, f32[32,8,128]{2,1,0:T(8,128)}) custom-call(bf16[16,144,128]{2,1,0:T(8,128)(2,1)S(1)} %all-to-all-done.held_ref, f32[18,128]{1,0:T(8,128)S(1)} %reshape.43.taps_ref), custom_call_target="tpu_custom_call" | custom-call | tf_op jit(solution)/shard_map/pallas_call | solution.py:38
  37.3 11.9 %all-to-all-start.1 = ((f32[32,8,128]{2,1,0:T(8,128)}), f32[32,8,128]{2,1,0:T(8,128)S(1)}, u32[]{:S(2)}, u32[]{:S(2)}) async-start(f32[32,8,128]{2,1,0:T(8,128)} %get-tuple-element.27), calls=%async_computation.1 | async-start | bytes 262144 | tf_op jit(solution)/shard_map/all_to_all | solution.py:24
  49.2 9.2 %all-to-all-done.1.sums_ref = f32[32,8,128]{2,1,0:T(8,128)S(1)} async-done(((f32[32,8,128]{2,1,0:T(8,128)}), f32[32,8,128]{2,1,0:T(8,128)S(1)}, u32[]{:S(2)}, u32[]{:S(2)}) %all-to-all-start.1) | async-done | bytes 131104 | tf_op jit(solution)/shard_map/all_to_all | solution.py:24
  60.1 8.4 %all-to-all-start.2 = ((bf16[16,144,256]{2,1,0:T(8,128)(2,1)}), bf16[16,144,256]{2,1,0:T(8,128)(2,1)S(1)}, u32[]{:S(2)}, u32[]{:S(2)}) async-start(bf16[16,144,256]{2,1,0:T(8,128)(2,1)} %get-tuple-element.28), calls=%async_computation.2 | async-start | bytes 2359296 | tf_op jit(solution)/shard_map/all_to_all | solution.py:24
  68.5 4.3 %collective-permute-start.3 = (bf16[4,144,256]{2,1,0:T(8,128)(2,1)}, bf16[4,144,256]{2,1,0:T(8,128)(2,1)S(1)}, u32[]{:S(2)}, u32[]{:S(2)}) collective-permute-start(bf16[4,144,256]{2,1,0:T(8,128)(2,1)} %get-tuple-element.30), channel_id=1, source_target_pairs={{0,8},{4,12},{8,16},{12,20},{16,24},{20,28},{24,0},{28,4},{1,9},{5... | collective-permute-start | bytes 884744 | tf_op jit(solution)/shard_map/ppermute | solution.py:29
  72.7 3.7 %collective-permute-start.4 = (bf16[4,144,256]{2,1,0:T(8,128)(2,1)}, bf16[4,144,256]{2,1,0:T(8,128)(2,1)}, u32[]{:S(2)}, u32[]{:S(2)}) collective-permute-start(bf16[4,144,256]{2,1,0:T(8,128)(2,1)} %get-tuple-element.31), channel_id=1, source_target_pairs={{0,24},{4,28},{8,0},{12,4},{16,8},{20,12},{24,16},{28,20},{1,25},{... | collective-permute-start | bytes 884744 | tf_op jit(solution)/shard_map/ppermute | solution.py:29
  76.4 30.7 %collective-permute-done.3.refs_3_ = bf16[4,144,256]{2,1,0:T(8,128)(2,1)S(1)} collective-permute-done((bf16[4,144,256]{2,1,0:T(8,128)(2,1)}, bf16[4,144,256]{2,1,0:T(8,128)(2,1)S(1)}, u32[]{:S(2)}, u32[]{:S(2)}) %collective-permute-start.3) | collective-permute-done | bytes 294944 | tf_op jit(solution)/shard_map/ppermute | solution.py:29
  107.8 5.1 %collective-permute-start.5 = (bf16[2,144,256]{2,1,0:T(8,128)(2,1)}, bf16[2,144,256]{2,1,0:T(8,128)(2,1)}, u32[]{:S(2)}, u32[]{:S(2)}) collective-permute-start(bf16[2,144,256]{2,1,0:T(8,128)(2,1)} %slice.12), channel_id=1, source_target_pairs={{0,4},{4,8},{8,12},{12,16},{16,20},{20,24},{24,28},{28,0},{1,5},{5... | collective-permute-start | bytes 442376 | tf_op jit(solution)/shard_map/ppermute | solution.py:29
  114.1 3.2 %collective-permute-done.5.refs_5_ = bf16[2,144,256]{2,1,0:T(8,128)(2,1)} collective-permute-done((bf16[2,144,256]{2,1,0:T(8,128)(2,1)}, bf16[2,144,256]{2,1,0:T(8,128)(2,1)}, u32[]{:S(2)}, u32[]{:S(2)}) %collective-permute-start.5) | collective-permute-done | bytes 147488 | tf_op jit(solution)/shard_map/ppermute | solution.py:29
  117.2 7.0 %shard_map.79 = (f32[2,16,144,128]{3,2,1,0:T(8,128)}, f32[136,256]{1,0:T(8,128)S(1)}, f32[136,256]{1,0:T(8,128)S(1)}) custom-call(s32[3]{0:T(128)S(1)} %pad_add_fusion.place_ref, bf16[2,16,144,128]{3,2,1,0:T(8,128)(2,1)S(1)} %get-tuple-element.23.z_ref, f32[8,128]{1,0:T(8,128)S(1)} %get-tuple-element.29.params_ref, ...), custom_call_target="tpu_custom_call" | custom-call | tf_op jit(solution)/shard_map/pallas_call | solution.py:38
  127.5 3.2 %collective-permute-start.7 = (f32[136,128]{1,0:T(8,128)S(1)}, f32[136,128]{1,0:T(8,128)S(1)}, u32[]{:S(2)}, u32[]{:S(2)}) collective-permute-start(f32[136,128]{1,0:T(8,128)S(1)} %constant_dynamic-slice_fusion), channel_id=1, source_target_pairs={{0,32},{32,0},{1,33},{33,1},{2,34},{34,2},{3,35},{35,3},{4,36},{36... | collective-permute-start | bytes 208904 | tf_op jit(solution)/shard_map/ppermute | solution.py:333
  130.7 3.0 %collective-permute-done.7 = f32[136,128]{1,0:T(8,128)S(1)} collective-permute-done((f32[136,128]{1,0:T(8,128)S(1)}, f32[136,128]{1,0:T(8,128)S(1)}, u32[]{:S(2)}, u32[]{:S(2)}) %collective-permute-start.7) | collective-permute-done | bytes 69664 | tf_op jit(solution)/shard_map/ppermute | solution.py:333
  133.8 11.2 %all_to_all.25.got_ref = f32[8,24,128]{2,1,0:T(8,128)S(1)} all-to-all(f32[8,24,128]{2,1,0:T(8,128)S(1)} %pad_maximum_fusion.3), channel_id=1, replica_groups=mesh['z'=8,'xl'=2,'y'=8,'xh'=2,'core'=2] {'z'}, dimensions={0} | all-to-all | bytes 196608 | tf_op jit(solution)/shard_map/all_to_all | solution.py:24
  145.0 5.2 %shard_map.81 = f32[32,24,128]{2,1,0:T(8,128)} custom-call(bf16[16,144,128]{2,1,0:T(8,128)(2,1)S(1)} %all-to-all-done.held_ref, bf16[2,16,144,128]{3,2,1,0:T(8,128)(2,1)S(1)} %get-tuple-element.23.z_ref, f32[8,128]{1,0:T(8,128)S(1)} %get-tuple-element.29.params_ref, f32[2,16,144,128]{3,2,1,0:T(8,128)} %get-tuple-element.35.dxhat_ref, ...), custom_call_target="tpu_custom_call" | custom-call | tf_op jit(solution)/shard_map/pallas_call | solution.py:38
  150.2 4.8 %all-to-all-start.4 = ((f32[32,24,128]{2,1,0:T(8,128)}), f32[32,24,128]{2,1,0:T(8,128)S(1)}, u32[]{:S(2)}, u32[]{:S(2)}) async-start(f32[32,24,128]{2,1,0:T(8,128)} %shard_map.81), calls=%async_computation.4 | async-start | bytes 786432 | tf_op jit(solution)/shard_map/all_to_all | solution.py:24
  155.0 3.0 %shard_map.80 = bf16[144,256]{1,0:T(8,128)(2,1)} custom-call(bf16[16,144,256]{2,1,0:T(8,128)(2,1)S(1)} %all-to-all-done.2.whole_ref, bf16[2048,512]{1,0:T(8,128)(2,1)} %maps_ref.1), custom_call_target="tpu_custom_call" | custom-call | tf_op jit(solution)/shard_map/pallas_call | solution.py:38
  157.9 12.0 %all-to-all-done.4.got_ref = f32[32,24,128]{2,1,0:T(8,128)S(1)} async-done(((f32[32,24,128]{2,1,0:T(8,128)}), f32[32,24,128]{2,1,0:T(8,128)S(1)}, u32[]{:S(2)}, u32[]{:S(2)}) %all-to-all-start.4) | async-done | bytes 393248 | tf_op jit(solution)/shard_map/all_to_all | solution.py:24
  (39 shorter events, 11.0 us)
Async XLA Ops:
  0.6 48.6 %copy-start = (f32[2,2048]{1,0:T(2,128)S(1)}, f32[2,2048]{1,0:T(2,128)}, u32[]{:S(2)}) copy-start(f32[2,2048]{1,0:T(2,128)} %param.8) | copy-start | bytes 49156
  0.6 12.1 %copy-start.5 = (bf16[1,2,72,256]{3,2,1,0:T(8,128)(2,1)S(1)}, bf16[1,2,72,256]{3,2,1,0:T(8,128)(2,1)}, u32[]{:S(2)}) copy-start(bf16[1,2,72,256]{3,2,1,0:T(8,128)(2,1)} %param.9) | copy-start | bytes 221188
  2.7 31.8 %all-to-all-start = ((bf16[16,144,128]{2,1,0:T(8,128)(2,1)}), bf16[16,144,128]{2,1,0:T(8,128)(2,1)S(1)}, u32[]{:S(2)}, u32[]{:S(2)}) async-start(bf16[16,144,128]{2,1,0:T(8,128)(2,1)} %shard_map.76), calls=%async_computation | async-start | bytes 1179648 | tf_op jit(solution)/shard_map/all_to_all | solution.py:24
  12.8 7.9 %collective-permute-start = (bf16[1,144,256]{2,1,0:T(8,128)(2,1)S(1)}, bf16[1,144,256]{2,1,0:T(8,128)(2,1)S(1)}, u32[]{:S(2)}, u32[]{:S(2)}) collective-permute-start(bf16[1,144,256]{2,1,0:T(8,128)(2,1)S(1)} %bitcast.23), channel_id=1, source_target_pairs={{0,2},{2,0},{1,3},{3,1},{4,6},{6,4},{5,7},{7,5},{8,10},{10,8},{9,1... | collective-permute-start | bytes 221192 | tf_op jit(solution)/shard_map/ppermute | solution.py:286
  20.7 13.8 %copy-start.2 = (bf16[2,144,256]{2,1,0:T(8,128)(2,1)}, bf16[2,144,256]{2,1,0:T(8,128)(2,1)S(1)}, u32[]{:S(2)}) copy-start(bf16[2,144,256]{2,1,0:T(8,128)(2,1)S(1)} %pad_maximum_fusion.2.refs_1_) | copy-start | bytes 442372
  20.7 9.7 %collective-permute-start.2 = (bf16[2,144,256]{2,1,0:T(8,128)(2,1)S(1)}, bf16[2,144,256]{2,1,0:T(8,128)(2,1)S(1)}, u32[]{:S(2)}, u32[]{:S(2)}) collective-permute-start(bf16[2,144,256]{2,1,0:T(8,128)(2,1)S(1)} %pad_maximum_fusion.2.refs_1_), channel_id=1, source_target_pairs={{0,28},{4,0},{8,4},{12,8},{16,12},{20,16},{24,20},{28,24},{1,29},{... | collective-permute-start | bytes 442376 | tf_op jit(solution)/shard_map/ppermute | solution.py:29
  25.4 8.2 %collective-permute-start.1 = (bf16[2,144,256]{2,1,0:T(8,128)(2,1)S(1)}, bf16[2,144,256]{2,1,0:T(8,128)(2,1)S(1)}, u32[]{:S(2)}, u32[]{:S(2)}) collective-permute-start(bf16[2,144,256]{2,1,0:T(8,128)(2,1)S(1)} %pad_maximum_fusion.2.refs_1_), channel_id=1, source_target_pairs={{0,4},{4,8},{8,12},{12,16},{16,20},{20,24},{24,28},{28,0},{1,5},{5... | collective-permute-start | bytes 442376 | tf_op jit(solution)/shard_map/ppermute | solution.py:29
  30.4 4.1 %copy-start.3 = (bf16[2,144,256]{2,1,0:T(8,128)(2,1)}, bf16[2,144,256]{2,1,0:T(8,128)(2,1)S(1)}, u32[]{:S(2)}) copy-start(bf16[2,144,256]{2,1,0:T(8,128)(2,1)S(1)} %collective-permute-done.2.refs_2_) | copy-start | bytes 442372
  33.6 0.9 copy-start.4
  37.3 21.2 %all-to-all-start.1 = ((f32[32,8,128]{2,1,0:T(8,128)}), f32[32,8,128]{2,1,0:T(8,128)S(1)}, u32[]{:S(2)}, u32[]{:S(2)}) async-start(f32[32,8,128]{2,1,0:T(8,128)} %get-tuple-element.27), calls=%async_computation.1 | async-start | bytes 262144 | tf_op jit(solution)/shard_map/all_to_all | solution.py:24
  60.1 73.7 %all-to-all-start.2 = ((bf16[16,144,256]{2,1,0:T(8,128)(2,1)}), bf16[16,144,256]{2,1,0:T(8,128)(2,1)S(1)}, u32[]{:S(2)}, u32[]{:S(2)}) async-start(bf16[16,144,256]{2,1,0:T(8,128)(2,1)} %get-tuple-element.28), calls=%async_computation.2 | async-start | bytes 2359296 | tf_op jit(solution)/shard_map/all_to_all | solution.py:24
  68.5 38.7 %collective-permute-start.3 = (bf16[4,144,256]{2,1,0:T(8,128)(2,1)}, bf16[4,144,256]{2,1,0:T(8,128)(2,1)S(1)}, u32[]{:S(2)}, u32[]{:S(2)}) collective-permute-start(bf16[4,144,256]{2,1,0:T(8,128)(2,1)} %get-tuple-element.30), channel_id=1, source_target_pairs={{0,8},{4,12},{8,16},{12,20},{16,24},{20,28},{24,0},{28,4},{1,9},{5... | collective-permute-start | bytes 884744 | tf_op jit(solution)/shard_map/ppermute | solution.py:29
  72.7 41.3 %collective-permute-start.4 = (bf16[4,144,256]{2,1,0:T(8,128)(2,1)}, bf16[4,144,256]{2,1,0:T(8,128)(2,1)}, u32[]{:S(2)}, u32[]{:S(2)}) collective-permute-start(bf16[4,144,256]{2,1,0:T(8,128)(2,1)} %get-tuple-element.31), channel_id=1, source_target_pairs={{0,24},{4,28},{8,0},{12,4},{16,8},{20,12},{24,16},{28,20},{1,25},{... | collective-permute-start | bytes 884744 | tf_op jit(solution)/shard_map/ppermute | solution.py:29
  107.1 10.1 %copy-start.1 = (bf16[4,144,256]{2,1,0:T(8,128)(2,1)}, bf16[4,144,256]{2,1,0:T(8,128)(2,1)S(1)}, u32[]{:S(2)}) copy-start(bf16[4,144,256]{2,1,0:T(8,128)(2,1)S(1)} %collective-permute-done.3.refs_3_) | copy-start | bytes 884740
  107.8 9.4 %collective-permute-start.5 = (bf16[2,144,256]{2,1,0:T(8,128)(2,1)}, bf16[2,144,256]{2,1,0:T(8,128)(2,1)}, u32[]{:S(2)}, u32[]{:S(2)}) collective-permute-start(bf16[2,144,256]{2,1,0:T(8,128)(2,1)} %slice.12), channel_id=1, source_target_pairs={{0,4},{4,8},{8,12},{12,16},{16,20},{20,24},{24,28},{28,0},{1,5},{5... | collective-permute-start | bytes 442376 | tf_op jit(solution)/shard_map/ppermute | solution.py:29
  124.2 3.2 %collective-permute-start.6 = (f32[136,256]{1,0:T(8,128)S(1)}, f32[136,256]{1,0:T(8,128)S(1)}, u32[]{:S(2)}, u32[]{:S(2)}) collective-permute-start(f32[136,256]{1,0:T(8,128)S(1)} %get-tuple-element.33), channel_id=1, source_target_pairs={{0,1},{1,0},{2,3},{3,2},{4,5},{5,4},{6,7},{7,6},{8,9},{9,8},{10,11... | collective-permute-start | bytes 417800 | tf_op jit(solution)/shard_map/ppermute | solution.py:329
  127.5 6.2 %collective-permute-start.7 = (f32[136,128]{1,0:T(8,128)S(1)}, f32[136,128]{1,0:T(8,128)S(1)}, u32[]{:S(2)}, u32[]{:S(2)}) collective-permute-start(f32[136,128]{1,0:T(8,128)S(1)} %constant_dynamic-slice_fusion), channel_id=1, source_target_pairs={{0,32},{32,0},{1,33},{33,1},{2,34},{34,2},{3,35},{35,3},{4,36},{36... | collective-permute-start | bytes 208904 | tf_op jit(solution)/shard_map/ppermute | solution.py:333
  150.2 19.8 %all-to-all-start.4 = ((f32[32,24,128]{2,1,0:T(8,128)}), f32[32,24,128]{2,1,0:T(8,128)S(1)}, u32[]{:S(2)}, u32[]{:S(2)}) async-start(f32[32,24,128]{2,1,0:T(8,128)} %shard_map.81), calls=%async_computation.4 | async-start | bytes 786432 | tf_op jit(solution)/shard_map/all_to_all | solution.py:24
where the time goes:
time: 171 us
  waiting for transfers between devices  70.9 us (41%)
  starting transfers between devices  61.9 us (36%)
  Pallas kernels  22.3 us (13%)
  blocking collectives  11.2 us (7%)
  local copies, waits for them, and re-layouts  1.84 us (1%)
  other arithmetic  1.73 us (1%)
    ppermute x5, waiting for transfers between devices, shifted(): lax.ppermute(value, 'y', [(i, (i + steps) % count) for i in range(count)])  39.5 us
    all_to_all x4, starting transfers between devices, exchange(): return lax.all_to_all(value, axes, 0, 0, tiled=True)  35.2 us
    pallas_call x7, Pallas kernels, call(): pl.pallas_call(kernel, out_shape=[pltpu.HBM(*o[:2]) if len(o) == 3 else j...  22.3 us
    all_to_all x4, waiting for transfers between devices, exchange(): return lax.all_to_all(value, axes, 0, 0, tiled=True)  21.2 us
    ppermute x5, starting transfers between devices, shifted(): lax.ppermute(value, 'y', [(i, (i + steps) % count) for i in range(count)])  19.6 us
    all_to_all x1, blocking collectives, exchange(): return lax.all_to_all(value, axes, 0, 0, tiled=True)  11.2 us
    ppermute x1, waiting for transfers between devices, body(): lax.ppermute(cot, 'xh', [(0, 1), (1, 0)])  5.87 us
  transfers between devices with their start and end apart: 12, of which 9 were waited for; matrix products, arithmetic and copies ran while one was open for 2% of the time, Pallas kernels for 6%

commit v1 on v0

--- a/solution.py
+++ b/solution.py
@@ -13,7 +13,7 @@
 eps_norm = 1e-05
 
 GROUP = ("y", "xh")
-ORDER = ((-1,), (0,), (1,), (-3, -2), (2, 3), (-4,))
+ORDER = (-3, -2, -1, 0, 1, 2, 3, -4)
 DP = ("z", "xl")
 ROWS = ("z", "xl", "core")
 f32 = jnp.float32
@@ -154,11 +154,10 @@
     rows, half = groups // 2, place_ref[1]
     zero = jnp.zeros((8, block), f32)
     total_ref[...] = jnp.zeros_like(total_ref)
-    for aparts, ref in zip(ORDER, pair_refs, strict=True):
-        for i, apart in enumerate(aparts):
+    for slot, ref in enumerate(pair_refs):
+        for i, apart in enumerate(ORDER):
             row = (place_ref[0] + apart + rows) % rows
-            for slot in range(2):
-                cots_ref[2 * row + (half ^ slot)] = ref[2 * i + slot]
+            cots_ref[2 * row + (half ^ slot)] = ref[i]
 
     def step(g, carry):
         carry = list(carry)
@@ -283,12 +282,13 @@
     (sent,) = call(pack_kernel, [((groups, pixels, block), bf16, None)], features.reshape(pixels, channels), slow=(0,))
     held = exchange(sent, GROUP)
     cot = cotangent.reshape(1, pixels, outs)
-    pairs = [jnp.concatenate([cot, lax.ppermute(cot, "xh", [(0, 1), (1, 0)])], axis=0)]
-    pair = pairs[0]
-    above, below = shifted(pair, 1), shifted(pair, -1)
-    left, right = jnp.concatenate([above, pair], axis=0), jnp.concatenate([pair, below], axis=0)
+    above = shifted(cot, 1)
+    below = shifted(cot, -1)
+    left = shifted(jnp.concatenate([above, cot], axis=0), 2)
+    right = shifted(jnp.concatenate([cot, below], axis=0), -2)
+    far = shifted(cot, 4)
     taps = lax.dynamic_slice_in_dim(depthwise, mine * block, block, 2).astype(f32).reshape(18, block)
-    held, left, right, taps = lax.optimization_barrier((held, left, right, taps))
+    held, taps = lax.optimization_barrier((held, taps))
     gain = lax.dynamic_slice_in_dim(bn_gain, mine * block, block, 1)
     maps = lax.dynamic_slice_in_dim(pointwise, mine * block, block, 0)
     maps = maps.reshape(block, 2, outs).transpose(2, 1, 0).reshape(outs, 2 * block)
@@ -300,11 +300,10 @@
         taps,
         scratch=[pad],
     )
-    sums, left, right = lax.optimization_barrier((sums, left, right))
     sums = exchange(sums, ROWS)
-    left = shifted(left, 2)
-    right = shifted(right, -2)
-    pairs = [above, pair, below, left, right, shifted(left[:2], 1)]
+    column = jnp.concatenate([left, above, cot, below, right, far], axis=0)
+    other = lax.ppermute(column, "xh", [(0, 1), (1, 0)])
+    pairs = [column, other]
     used, params = call(
         functools.partial(norm_kernel, count),
         [((groups, pixels, 2 * block), bf16, None), ((8, block), f32)],

time: 171 us -> 174 us (1.018)
  local copies, waits for them, and re-layouts: 1.84 us -> 5.04 us
    ppermute x5, waiting for transfers between devices: 39.5 us -> 21.6 us  [shifted(): lax.ppermute(value, 'y', [(i, (i + steps) % count) for i in range(count)])]
    all_to_all x4, waiting for transfers between devices: 21.2 us -> 32.1 us  [exchange(): return lax.all_to_all(value, axes, 0, 0, tiled=True)]
    ppermute x1, waiting for transfers between devices: 5.87 us -> 12.5 us  [body(): other = lax.ppermute(column, 'xh', [(0, 1), (1, 0)])]
    unnamed x13 -> x10, local copies, waits for them, and re-layouts: 0.15 us -> 3.39 us
    all_to_all x4, starting transfers between devices: 35.2 us -> 32.7 us  [exchange(): return lax.all_to_all(value, axes, 0, 0, tiled=True)]
  transfers between devices with their start and end apart: 12 -> 12, of which waited for: 9 -> 8; matrix products, arithmetic and copies ran while one was open for 2% -> 3% of each run, Pallas kernels for 6% -> 7%
where the time goes in v1:
time: 174 us; the launch traced here: 173 us
  waiting for transfers between devices  71.4 us (41%)
  starting transfers between devices  60.6 us (35%)
  Pallas kernels  22.3 us (13%)
  blocking collectives  12.1 us (7%)
  local copies, waits for them, and re-layouts  5.04 us (3%)
    all_to_all x4, starting transfers between devices, exchange(): return lax.all_to_all(value, axes, 0, 0, tiled=True)  32.7 us
    all_to_all x4, waiting for transfers between devices, exchange(): return lax.all_to_all(value, axes, 0, 0, tiled=True)  32.1 us
    pallas_call x7, Pallas kernels, call(): pl.pallas_call(kernel, out_shape=[pltpu.HBM(*o[:2]) if len(o) == 3 else j...  22.3 us
    ppermute x5, waiting for transfers between devices, shifted(): lax.ppermute(value, 'y', [(i, (i + steps) % count) for i in range(count)])  21.6 us
    ppermute x5, starting transfers between devices, shifted(): lax.ppermute(value, 'y', [(i, (i + steps) % count) for i in range(count)])  21.1 us
    ppermute x1, waiting for transfers between devices, body(): other = lax.ppermute(column, 'xh', [(0, 1), (1, 0)])  12.5 us
    all_to_all x1, blocking collectives, exchange(): return lax.all_to_all(value, axes, 0, 0, tiled=True)  12.1 us
    ppermute x1, waiting for transfers between devices, body(): keep = keep + lax.ppermute(sent, 'xl', [(0, 1), (1, 0)])  3.8 us
  transfers between devices with their start and end apart: 12, of which 8 were waited for; matrix products, arithmetic and copies ran while one was open for 3% of the time, Pallas kernels for 7%

profile of v1, /device:TPU:6, one launch (start us, length us, event | category | flops | bytes accessed | tf_op | source)
XLA Modules:
  0.0 173.1 jit_solution(10439644175613475803)
XLA Ops:
  0.7 2.0 %shard_map.76 = bf16[16,144,128]{2,1,0:T(8,128)(2,1)} custom-call(bf16[144,2048]{1,0:T(8,128)(2,1)} %bitcast.21), custom_call_target="tpu_custom_call" | custom-call | tf_op jit(solution)/shard_map/pallas_call | solution.py:38
  2.7 10.1 %all-to-all-start = ((bf16[16,144,128]{2,1,0:T(8,128)(2,1)}), bf16[16,144,128]{2,1,0:T(8,128)(2,1)S(1)}, u32[]{:S(2)}, u32[]{:S(2)}) async-start(bf16[16,144,128]{2,1,0:T(8,128)(2,1)} %shard_map.76), calls=%async_computation | async-start | bytes 1179648 | tf_op jit(solution)/shard_map/all_to_all | solution.py:24
  13.5 16.8 %all-to-all-done.held_ref = bf16[16,144,128]{2,1,0:T(8,128)(2,1)S(1)} async-done(((bf16[16,144,128]{2,1,0:T(8,128)(2,1)}), bf16[16,144,128]{2,1,0:T(8,128)(2,1)S(1)}, u32[]{:S(2)}, u32[]{:S(2)}) %all-to-all-start) | async-done | bytes 589856 | tf_op jit(solution)/shard_map/all_to_all | solution.py:24
  30.2 2.7 %shard_map.77 = (bf16[2,16,144,128]{3,2,1,0:T(8,128)(2,1)S(1)}, f32[32,8,128]{2,1,0:T(8,128)}) custom-call(bf16[16,144,128]{2,1,0:T(8,128)(2,1)S(1)} %all-to-all-done.held_ref, f32[18,128]{1,0:T(8,128)S(1)} %reshape.43.taps_ref), custom_call_target="tpu_custom_call" | custom-call | tf_op jit(solution)/shard_map/pallas_call | solution.py:38
  33.0 11.9 %all-to-all-start.1 = ((f32[32,8,128]{2,1,0:T(8,128)}), f32[32,8,128]{2,1,0:T(8,128)S(1)}, u32[]{:S(2)}, u32[]{:S(2)}) async-start(f32[32,8,128]{2,1,0:T(8,128)} %get-tuple-element.19), calls=%async_computation.1 | async-start | bytes 262144 | tf_op jit(solution)/shard_map/all_to_all | solution.py:24
  44.9 1.9 %collective-permute-start.2 = (bf16[1,144,256]{2,1,0:T(8,128)(2,1)S(1)}, bf16[1,144,256]{2,1,0:T(8,128)(2,1)S(1)}, u32[]{:S(2)}, u32[]{:S(2)}) collective-permute-start(bf16[1,144,256]{2,1,0:T(8,128)(2,1)S(1)} %bitcast.23), channel_id=1, source_target_pairs={{0,28},{4,0},{8,4},{12,8},{16,12},{20,16},{24,20},{28,24},{1,29},{... | collective-permute-start | bytes 221192 | tf_op jit(solution)/shard_map/ppermute | solution.py:29
  46.8 3.9 %collective-permute-start = (bf16[1,144,256]{2,1,0:T(8,128)(2,1)S(1)}, bf16[1,144,256]{2,1,0:T(8,128)(2,1)S(1)}, u32[]{:S(2)}, u32[]{:S(2)}) collective-permute-start(bf16[1,144,256]{2,1,0:T(8,128)(2,1)S(1)} %bitcast.24), channel_id=1, source_target_pairs={{0,4},{4,8},{8,12},{12,16},{16,20},{20,24},{24,28},{28,0},{1,5},{5... | collective-permute-start | bytes 221192 | tf_op jit(solution)/shard_map/ppermute | solution.py:29
  50.8 3.3 %all-to-all-done.1.sums_ref = f32[32,8,128]{2,1,0:T(8,128)S(1)} async-done(((f32[32,8,128]{2,1,0:T(8,128)}), f32[32,8,128]{2,1,0:T(8,128)S(1)}, u32[]{:S(2)}, u32[]{:S(2)}) %all-to-all-start.1) | async-done | bytes 131104 | tf_op jit(solution)/shard_map/all_to_all | solution.py:24
  55.8 6.5 %all-to-all-start.2 = ((bf16[16,144,256]{2,1,0:T(8,128)(2,1)}), bf16[16,144,256]{2,1,0:T(8,128)(2,1)S(1)}, u32[]{:S(2)}, u32[]{:S(2)}) async-start(bf16[16,144,256]{2,1,0:T(8,128)(2,1)} %get-tuple-element.20), calls=%async_computation.2 | async-start | bytes 2359296 | tf_op jit(solution)/shard_map/all_to_all | solution.py:24
  62.4 4.3 %collective-permute-start.1 = (bf16[2,144,256]{2,1,0:T(8,128)(2,1)S(1)}, bf16[2,144,256]{2,1,0:T(8,128)(2,1)S(1)}, u32[]{:S(2)}, u32[]{:S(2)}) collective-permute-start(bf16[2,144,256]{2,1,0:T(8,128)(2,1)S(1)} %get-tuple-element.30), channel_id=1, source_target_pairs={{0,8},{4,12},{8,16},{12,20},{16,24},{20,28},{24,0},{28,4},{1,9},{5... | collective-permute-start | bytes 442376 | tf_op jit(solution)/shard_map/ppermute | solution.py:29
  66.7 5.5 %collective-permute-start.4 = (bf16[1,144,256]{2,1,0:T(8,128)(2,1)S(1)}, bf16[1,144,256]{2,1,0:T(8,128)(2,1)S(1)}, u32[]{:S(2)}, u32[]{:S(2)}) collective-permute-start(bf16[1,144,256]{2,1,0:T(8,128)(2,1)S(1)} %bitcast.26), channel_id=1, source_target_pairs={{0,16},{4,20},{8,24},{12,28},{16,0},{20,4},{24,8},{28,12},{1,17},{... | collective-permute-start | bytes 221192 | tf_op jit(solution)/shard_map/ppermute | solution.py:29
  72.2 5.5 %collective-permute-start.3 = (bf16[2,144,256]{2,1,0:T(8,128)(2,1)S(1)}, bf16[2,144,256]{2,1,0:T(8,128)(2,1)S(1)}, u32[]{:S(2)}, u32[]{:S(2)}) collective-permute-start(bf16[2,144,256]{2,1,0:T(8,128)(2,1)S(1)} %get-tuple-element.29), channel_id=1, source_target_pairs={{0,24},{4,28},{8,0},{12,4},{16,8},{20,12},{24,16},{28,20},{1,25},{... | collective-permute-start | bytes 442376 | tf_op jit(solution)/shard_map/ppermute | solution.py:29
  77.7 20.9 %collective-permute-done.1 = bf16[2,144,256]{2,1,0:T(8,128)(2,1)S(1)} collective-permute-done((bf16[2,144,256]{2,1,0:T(8,128)(2,1)S(1)}, bf16[2,144,256]{2,1,0:T(8,128)(2,1)S(1)}, u32[]{:S(2)}, u32[]{:S(2)}) %collective-permute-start.1) | collective-permute-done | bytes 147488 | tf_op jit(solution)/shard_map/ppermute | solution.py:29
  103.2 2.5 %collective-permute-start.5 = (bf16[8,144,256]{2,1,0:T(8,128)(2,1)}, bf16[8,144,256]{2,1,0:T(8,128)(2,1)}, u32[]{:S(2)}, u32[]{:S(2)}) collective-permute-start(bf16[8,144,256]{2,1,0:T(8,128)(2,1)} %constant_dynamic-update-slice_fusion.refs_0_), channel_id=1, source_target_pairs={{0,2},{2,0},{1,3},{3,1},{4,6},{6,4},{5,7},{7,5},{8,10},{10,8},{9,1... | collective-permute-start | bytes 1769480 | tf_op jit(solution)/shard_map/ppermute | solution.py:305
  106.8 12.5 %collective-permute-done.5.refs_1_ = bf16[8,144,256]{2,1,0:T(8,128)(2,1)} collective-permute-done((bf16[8,144,256]{2,1,0:T(8,128)(2,1)}, bf16[8,144,256]{2,1,0:T(8,128)(2,1)}, u32[]{:S(2)}, u32[]{:S(2)}) %collective-permute-start.5) | collective-permute-done | bytes 589856 | tf_op jit(solution)/shard_map/ppermute | solution.py:305
  119.4 7.0 %shard_map.79 = (f32[2,16,144,128]{3,2,1,0:T(8,128)}, f32[136,256]{1,0:T(8,128)S(1)}, f32[136,256]{1,0:T(8,128)S(1)}) custom-call(s32[3]{0:T(128)S(1)} %pad_add_fusion.place_ref, bf16[2,16,144,128]{3,2,1,0:T(8,128)(2,1)S(1)} %get-tuple-element.18.z_ref, f32[8,128]{1,0:T(8,128)S(1)} %get-tuple-element.21.params_ref, ...), custom_call_target="tpu_custom_call" | custom-call | tf_op jit(solution)/shard_map/pallas_call | solution.py:38
  126.4 1.9 %collective-permute-start.6 = (f32[136,256]{1,0:T(8,128)S(1)}, f32[136,256]{1,0:T(8,128)S(1)}, u32[]{:S(2)}, u32[]{:S(2)}) collective-permute-start(f32[136,256]{1,0:T(8,128)S(1)} %get-tuple-element.23), channel_id=1, source_target_pairs={{0,1},{1,0},{2,3},{3,2},{4,5},{5,4},{6,7},{7,6},{8,9},{9,8},{10,11... | collective-permute-start | bytes 417800 | tf_op jit(solution)/shard_map/ppermute | solution.py:328
  129.6 2.4 %collective-permute-start.7 = (f32[136,128]{1,0:T(8,128)S(1)}, f32[136,128]{1,0:T(8,128)S(1)}, u32[]{:S(2)}, u32[]{:S(2)}) collective-permute-start(f32[136,128]{1,0:T(8,128)S(1)} %constant_dynamic-slice_fusion), channel_id=1, source_target_pairs={{0,32},{32,0},{1,33},{33,1},{2,34},{34,2},{3,35},{35,3},{4,36},{36... | collective-permute-start | bytes 208904 | tf_op jit(solution)/shard_map/ppermute | solution.py:332
  132.1 3.8 %collective-permute-done.7 = f32[136,128]{1,0:T(8,128)S(1)} collective-permute-done((f32[136,128]{1,0:T(8,128)S(1)}, f32[136,128]{1,0:T(8,128)S(1)}, u32[]{:S(2)}, u32[]{:S(2)}) %collective-permute-start.7) | collective-permute-done | bytes 69664 | tf_op jit(solution)/shard_map/ppermute | solution.py:332
  135.9 12.1 %all_to_all.25.got_ref = f32[8,24,128]{2,1,0:T(8,128)S(1)} all-to-all(f32[8,24,128]{2,1,0:T(8,128)S(1)} %pad_maximum_fusion.2), channel_id=1, replica_groups=mesh['z'=8,'xl'=2,'y'=8,'xh'=2,'core'=2] {'z'}, dimensions={0} | all-to-all | bytes 196608 | tf_op jit(solution)/shard_map/all_to_all | solution.py:24
  148.0 5.2 %shard_map.81 = f32[32,24,128]{2,1,0:T(8,128)} custom-call(bf16[16,144,128]{2,1,0:T(8,128)(2,1)S(1)} %all-to-all-done.held_ref, bf16[2,16,144,128]{3,2,1,0:T(8,128)(2,1)S(1)} %get-tuple-element.18.z_ref, f32[8,128]{1,0:T(8,128)S(1)} %get-tuple-element.21.params_ref, f32[2,16,144,128]{3,2,1,0:T(8,128)} %get-tuple-element.25.dxhat_ref, ...), custom_call_target="tpu_custom_call" | custom-call | tf_op jit(solution)/shard_map/pallas_call | solution.py:38
  153.3 4.1 %all-to-all-start.4 = ((f32[32,24,128]{2,1,0:T(8,128)}), f32[32,24,128]{2,1,0:T(8,128)S(1)}, u32[]{:S(2)}, u32[]{:S(2)}) async-start(f32[32,24,128]{2,1,0:T(8,128)} %shard_map.81), calls=%async_computation.4 | async-start | bytes 786432 | tf_op jit(solution)/shard_map/all_to_all | solution.py:24
  157.4 3.0 %shard_map.80 = bf16[144,256]{1,0:T(8,128)(2,1)} custom-call(bf16[16,144,256]{2,1,0:T(8,128)(2,1)S(1)} %all-to-all-done.2.whole_ref, bf16[2048,512]{1,0:T(8,128)(2,1)} %maps_ref.1), custom_call_target="tpu_custom_call" | custom-call | tf_op jit(solution)/shard_map/pallas_call | solution.py:38
  160.4 12.0 %all-to-all-done.4.got_ref = f32[32,24,128]{2,1,0:T(8,128)S(1)} async-done(((f32[32,24,128]{2,1,0:T(8,128)}), f32[32,24,128]{2,1,0:T(8,128)S(1)}, u32[]{:S(2)}, u32[]{:S(2)}) %all-to-all-start.4) | async-done | bytes 393248 | tf_op jit(solution)/shard_map/all_to_all | solution.py:24
  (35 shorter events, 10.3 us)
Async XLA Ops:
  0.6 50.1 %copy-start = (f32[2,2048]{1,0:T(2,128)S(1)}, f32[2,2048]{1,0:T(2,128)}, u32[]{:S(2)}) copy-start(f32[2,2048]{1,0:T(2,128)} %param.8) | copy-start | bytes 49156
  0.6 44.3 %copy-start.1 = (bf16[1,2,72,256]{3,2,1,0:T(8,128)(2,1)S(1)}, bf16[1,2,72,256]{3,2,1,0:T(8,128)(2,1)}, u32[]{:S(2)}) copy-start(bf16[1,2,72,256]{3,2,1,0:T(8,128)(2,1)} %param.9) | copy-start | bytes 221188
  2.7 27.6 %all-to-all-start = ((bf16[16,144,128]{2,1,0:T(8,128)(2,1)}), bf16[16,144,128]{2,1,0:T(8,128)(2,1)S(1)}, u32[]{:S(2)}, u32[]{:S(2)}) async-start(bf16[16,144,128]{2,1,0:T(8,128)(2,1)} %shard_map.76), calls=%async_computation | async-start | bytes 1179648 | tf_op jit(solution)/shard_map/all_to_all | solution.py:24
  33.0 21.2 %all-to-all-start.1 = ((f32[32,8,128]{2,1,0:T(8,128)}), f32[32,8,128]{2,1,0:T(8,128)S(1)}, u32[]{:S(2)}, u32[]{:S(2)}) async-start(f32[32,8,128]{2,1,0:T(8,128)} %get-tuple-element.19), calls=%async_computation.1 | async-start | bytes 262144 | tf_op jit(solution)/shard_map/all_to_all | solution.py:24
  44.9 17.4 %collective-permute-start.2 = (bf16[1,144,256]{2,1,0:T(8,128)(2,1)S(1)}, bf16[1,144,256]{2,1,0:T(8,128)(2,1)S(1)}, u32[]{:S(2)}, u32[]{:S(2)}) collective-permute-start(bf16[1,144,256]{2,1,0:T(8,128)(2,1)S(1)} %bitcast.23), channel_id=1, source_target_pairs={{0,28},{4,0},{8,4},{12,8},{16,12},{20,16},{24,20},{28,24},{1,29},{... | collective-permute-start | bytes 221192 | tf_op jit(solution)/shard_map/ppermute | solution.py:29
  46.8 15.5 %collective-permute-start = (bf16[1,144,256]{2,1,0:T(8,128)(2,1)S(1)}, bf16[1,144,256]{2,1,0:T(8,128)(2,1)S(1)}, u32[]{:S(2)}, u32[]{:S(2)}) collective-permute-start(bf16[1,144,256]{2,1,0:T(8,128)(2,1)S(1)} %bitcast.24), channel_id=1, source_target_pairs={{0,4},{4,8},{8,12},{12,16},{16,20},{20,24},{24,28},{28,0},{1,5},{5... | collective-permute-start | bytes 221192 | tf_op jit(solution)/shard_map/ppermute | solution.py:29
  55.8 80.2 %all-to-all-start.2 = ((bf16[16,144,256]{2,1,0:T(8,128)(2,1)}), bf16[16,144,256]{2,1,0:T(8,128)(2,1)S(1)}, u32[]{:S(2)}, u32[]{:S(2)}) async-start(bf16[16,144,256]{2,1,0:T(8,128)(2,1)} %get-tuple-element.20), calls=%async_computation.2 | async-start | bytes 2359296 | tf_op jit(solution)/shard_map/all_to_all | solution.py:24
  62.4 36.2 %collective-permute-start.1 = (bf16[2,144,256]{2,1,0:T(8,128)(2,1)S(1)}, bf16[2,144,256]{2,1,0:T(8,128)(2,1)S(1)}, u32[]{:S(2)}, u32[]{:S(2)}) collective-permute-start(bf16[2,144,256]{2,1,0:T(8,128)(2,1)S(1)} %get-tuple-element.30), channel_id=1, source_target_pairs={{0,8},{4,12},{8,16},{12,20},{16,24},{20,28},{24,0},{28,4},{1,9},{5... | collective-permute-start | bytes 442376 | tf_op jit(solution)/shard_map/ppermute | solution.py:29
  66.7 35.9 %collective-permute-start.4 = (bf16[1,144,256]{2,1,0:T(8,128)(2,1)S(1)}, bf16[1,144,256]{2,1,0:T(8,128)(2,1)S(1)}, u32[]{:S(2)}, u32[]{:S(2)}) collective-permute-start(bf16[1,144,256]{2,1,0:T(8,128)(2,1)S(1)} %bitcast.26), channel_id=1, source_target_pairs={{0,16},{4,20},{8,24},{12,28},{16,0},{20,4},{24,8},{28,12},{1,17},{... | collective-permute-start | bytes 221192 | tf_op jit(solution)/shard_map/ppermute | solution.py:29
  72.2 28.9 %collective-permute-start.3 = (bf16[2,144,256]{2,1,0:T(8,128)(2,1)S(1)}, bf16[2,144,256]{2,1,0:T(8,128)(2,1)S(1)}, u32[]{:S(2)}, u32[]{:S(2)}) collective-permute-start(bf16[2,144,256]{2,1,0:T(8,128)(2,1)S(1)} %get-tuple-element.29), channel_id=1, source_target_pairs={{0,24},{4,28},{8,0},{12,4},{16,8},{20,12},{24,16},{28,20},{1,25},{... | collective-permute-start | bytes 442376 | tf_op jit(solution)/shard_map/ppermute | solution.py:29
  103.2 16.2 %collective-permute-start.5 = (bf16[8,144,256]{2,1,0:T(8,128)(2,1)}, bf16[8,144,256]{2,1,0:T(8,128)(2,1)}, u32[]{:S(2)}, u32[]{:S(2)}) collective-permute-start(bf16[8,144,256]{2,1,0:T(8,128)(2,1)} %constant_dynamic-update-slice_fusion.refs_0_), channel_id=1, source_target_pairs={{0,2},{2,0},{1,3},{3,1},{4,6},{6,4},{5,7},{7,5},{8,10},{10,8},{9,1... | collective-permute-start | bytes 1769480 | tf_op jit(solution)/shard_map/ppermute | solution.py:305
  126.4 3.2 %collective-permute-start.6 = (f32[136,256]{1,0:T(8,128)S(1)}, f32[136,256]{1,0:T(8,128)S(1)}, u32[]{:S(2)}, u32[]{:S(2)}) collective-permute-start(f32[136,256]{1,0:T(8,128)S(1)} %get-tuple-element.23), channel_id=1, source_target_pairs={{0,1},{1,0},{2,3},{3,2},{4,5},{5,4},{6,7},{7,6},{8,9},{9,8},{10,11... | collective-permute-start | bytes 417800 | tf_op jit(solution)/shard_map/ppermute | solution.py:328
  129.6 6.2 %collective-permute-start.7 = (f32[136,128]{1,0:T(8,128)S(1)}, f32[136,128]{1,0:T(8,128)S(1)}, u32[]{:S(2)}, u32[]{:S(2)}) collective-permute-start(f32[136,128]{1,0:T(8,128)S(1)} %constant_dynamic-slice_fusion), channel_id=1, source_target_pairs={{0,32},{32,0},{1,33},{33,1},{2,34},{34,2},{3,35},{35,3},{4,36},{36... | collective-permute-start | bytes 208904 | tf_op jit(solution)/shard_map/ppermute | solution.py:332
  153.3 19.1 %all-to-all-start.4 = ((f32[32,24,128]{2,1,0:T(8,128)}), f32[32,24,128]{2,1,0:T(8,128)S(1)}, u32[]{:S(2)}, u32[]{:S(2)}) async-start(f32[32,24,128]{2,1,0:T(8,128)} %shard_map.81), calls=%async_computation.4 | async-start | bytes 786432 | tf_op jit(solution)/shard_map/all_to_all | solution.py:24

commit v2 on v1

--- a/solution.py
+++ b/solution.py
@@ -13,7 +13,7 @@
 eps_norm = 1e-05
 
 GROUP = ("y", "xh")
-ORDER = (-3, -2, -1, 0, 1, 2, 3, -4)
+ORDER = (-4, -3, -2, -1, 0, 1, 2, 3)
 DP = ("z", "xl")
 ROWS = ("z", "xl", "core")
 f32 = jnp.float32
@@ -51,6 +51,12 @@
         out_ref[g] = feat_ref[:, g * block : (g + 1) * block]
 
 
+def column_kernel(left_ref, near_ref, right_ref, out_ref):
+    out_ref[:3] = left_ref[...]
+    out_ref[3:6] = near_ref[...]
+    out_ref[6:] = right_ref[...]
+
+
 def fill_padded(held_ref, pad):
     groups = held_ref.shape[0]
     total, rows, wide, block = pad.shape
@@ -113,7 +119,7 @@
     for i, s in enumerate(sums):
         tile = jnp.where(line == i, s, tile)
     for i in range(sums_ref.shape[0]):
-        sums_ref[i] = tile
+        sums_ref[i] = tile[:4]
 
 
 def norm_kernel(count, z_ref, sums_ref, gain_ref, used_ref, params_ref):
@@ -284,9 +290,9 @@
     cot = cotangent.reshape(1, pixels, outs)
     above = shifted(cot, 1)
     below = shifted(cot, -1)
-    left = shifted(jnp.concatenate([above, cot], axis=0), 2)
-    right = shifted(jnp.concatenate([cot, below], axis=0), -2)
-    far = shifted(cot, 4)
+    near = jnp.concatenate([above, cot, below], axis=0)
+    left = shifted(near, 3)
+    right = shifted(near[:2], -3)
     taps = lax.dynamic_slice_in_dim(depthwise, mine * block, block, 2).astype(f32).reshape(18, block)
     held, taps = lax.optimization_barrier((held, taps))
     gain = lax.dynamic_slice_in_dim(bn_gain, mine * block, block, 1)
@@ -295,13 +301,13 @@
 
     z, sums = call(
         functools.partial(forward_kernel, row_step),
-        [((2, groups, pixels, block), bf16), ((peers, 8, block), f32, None)],
+        [((2, groups, pixels, block), bf16), ((peers, 4, block), f32, None)],
         held,
         taps,
         scratch=[pad],
     )
     sums = exchange(sums, ROWS)
-    column = jnp.concatenate([left, above, cot, below, right, far], axis=0)
+    (column,) = call(column_kernel, [((8, pixels, outs), bf16, None)], left, near, right)
     other = lax.ppermute(column, "xh", [(0, 1), (1, 0)])
     pairs = [column, other]
     used, params = call(

time: 174 us -> 185 us (1.063)
  waiting for transfers between devices: 71.4 us -> 90.1 us
  starting transfers between devices: 60.6 us -> 56 us
  local copies, waits for them, and re-layouts: 5.04 us -> 1.14 us
    ppermute x5 -> x4, waiting for transfers between devices: 21.6 us -> 33.9 us  [shifted(): lax.ppermute(value, 'y', [(i, (i + steps) % count) for i in range(count)])]
    ppermute x5 -> x4, starting transfers between devices: 21.1 us -> 15.4 us  [shifted(): lax.ppermute(value, 'y', [(i, (i + steps) % count) for i in range(count)])]
    all_to_all x4, waiting for transfers between devices: 32.1 us -> 36.5 us  [exchange(): return lax.all_to_all(value, axes, 0, 0, tiled=True)]
    unnamed x10 -> x5, local copies, waits for them, and re-layouts: 3.39 us -> 0.13 us
    ppermute x1, waiting for transfers between devices: 12.5 us -> 15.1 us  [body(): other = lax.ppermute(column, 'xh', [(0, 1), (1, 0)])]
    pallas_call x7 -> x8, Pallas kernels: 22.3 us -> 23.1 us  [call(): pl.pallas_call(kernel, out_shape=[pltpu.HBM(*o[:2]) if len(o) == 3 else j...]
  transfers between devices with their start and end apart: 12 -> 11, of which waited for: 8 -> 10; matrix products, arithmetic and copies ran while one was open for 3% -> 1% of each run, Pallas kernels for 7% -> 6%
where the time goes in v2:
time: 185 us; the launch traced here: 183 us
  waiting for transfers between devices  90.1 us (49%)
  starting transfers between devices  56 us (30%)
  Pallas kernels  23.1 us (12%)
  blocking collectives  11.1 us (6%)
    all_to_all x4, waiting for transfers between devices, exchange(): return lax.all_to_all(value, axes, 0, 0, tiled=True)  36.5 us
    ppermute x4, waiting for transfers between devices, shifted(): lax.ppermute(value, 'y', [(i, (i + steps) % count) for i in range(count)])  33.9 us
    all_to_all x4, starting transfers between devices, exchange(): return lax.all_to_all(value, axes, 0, 0, tiled=True)  33.1 us
    pallas_call x8, Pallas kernels, call(): pl.pallas_call(kernel, out_shape=[pltpu.HBM(*o[:2]) if len(o) == 3 else j...  23.1 us
    ppermute x4, starting transfers between devices, shifted(): lax.ppermute(value, 'y', [(i, (i + steps) % count) for i in range(count)])  15.4 us
    ppermute x1, waiting for transfers between devices, body(): other = lax.ppermute(column, 'xh', [(0, 1), (1, 0)])  15.1 us
    all_to_all x1, blocking collectives, exchange(): return lax.all_to_all(value, axes, 0, 0, tiled=True)  11.1 us
  transfers between devices with their start and end apart: 11, of which 10 were waited for; matrix products, arithmetic and copies ran while one was open for 1% of the time, Pallas kernels for 6%

profile of v2, /device:TPU:6, one launch (start us, length us, event | category | flops | bytes accessed | tf_op | source)
XLA Modules:
  0.0 183.2 jit_solution(10276714637091224273)
XLA Ops:
  0.6 2.0 %shard_map.76 = bf16[16,144,128]{2,1,0:T(8,128)(2,1)} custom-call(bf16[144,2048]{1,0:T(8,128)(2,1)} %bitcast.21), custom_call_target="tpu_custom_call" | custom-call | tf_op jit(solution)/shard_map/pallas_call | solution.py:38
  2.6 10.1 %all-to-all-start = ((bf16[16,144,128]{2,1,0:T(8,128)(2,1)}), bf16[16,144,128]{2,1,0:T(8,128)(2,1)S(1)}, u32[]{:S(2)}, u32[]{:S(2)}) async-start(bf16[16,144,128]{2,1,0:T(8,128)(2,1)} %shard_map.76), calls=%async_computation | async-start | bytes 1179648 | tf_op jit(solution)/shard_map/all_to_all | solution.py:24
  13.4 16.8 %all-to-all-done.held_ref = bf16[16,144,128]{2,1,0:T(8,128)(2,1)S(1)} async-done(((bf16[16,144,128]{2,1,0:T(8,128)(2,1)}), bf16[16,144,128]{2,1,0:T(8,128)(2,1)S(1)}, u32[]{:S(2)}, u32[]{:S(2)}) %all-to-all-start) | async-done | bytes 589856 | tf_op jit(solution)/shard_map/all_to_all | solution.py:24
  30.2 2.7 %shard_map.77 = (bf16[2,16,144,128]{3,2,1,0:T(8,128)(2,1)S(1)}, f32[32,4,128]{2,1,0:T(4,128)}) custom-call(bf16[16,144,128]{2,1,0:T(8,128)(2,1)S(1)} %all-to-all-done.held_ref, f32[18,128]{1,0:T(8,128)S(1)} %reshape.43.taps_ref), custom_call_target="tpu_custom_call" | custom-call | tf_op jit(solution)/shard_map/pallas_call | solution.py:38
  32.9 11.9 %all-to-all-start.1 = ((f32[32,4,128]{2,1,0:T(4,128)}), f32[32,4,128]{2,1,0:T(4,128)S(1)}, u32[]{:S(2)}, u32[]{:S(2)}) async-start(f32[32,4,128]{2,1,0:T(4,128)} %get-tuple-element.19), calls=%async_computation.1 | async-start | bytes 131072 | tf_op jit(solution)/shard_map/all_to_all | solution.py:24
  44.9 7.8 %all-to-all-done.1.sums_ref = f32[32,4,128]{2,1,0:T(4,128)S(1)} async-done(((f32[32,4,128]{2,1,0:T(4,128)}), f32[32,4,128]{2,1,0:T(4,128)S(1)}, u32[]{:S(2)}, u32[]{:S(2)}) %all-to-all-start.1) | async-done | bytes 65568 | tf_op jit(solution)/shard_map/all_to_all | solution.py:24
  54.3 6.5 %all-to-all-start.2 = ((bf16[16,144,256]{2,1,0:T(8,128)(2,1)}), bf16[16,144,256]{2,1,0:T(8,128)(2,1)S(1)}, u32[]{:S(2)}, u32[]{:S(2)}) async-start(bf16[16,144,256]{2,1,0:T(8,128)(2,1)} %get-tuple-element.20), calls=%async_computation.2 | async-start | bytes 2359296 | tf_op jit(solution)/shard_map/all_to_all | solution.py:24
  60.9 4.7 %collective-permute-start.1 = (bf16[1,144,256]{2,1,0:T(8,128)(2,1)S(1)}, bf16[1,144,256]{2,1,0:T(8,128)(2,1)S(1)}, u32[]{:S(2)}, u32[]{:S(2)}) collective-permute-start(bf16[1,144,256]{2,1,0:T(8,128)(2,1)S(1)} %bitcast.23), channel_id=1, source_target_pairs={{0,28},{4,0},{8,4},{12,8},{16,12},{20,16},{24,20},{28,24},{1,29},{... | collective-permute-start | bytes 221192 | tf_op jit(solution)/shard_map/ppermute | solution.py:29
  65.6 1.9 %collective-permute-start = (bf16[1,144,256]{2,1,0:T(8,128)(2,1)S(1)}, bf16[1,144,256]{2,1,0:T(8,128)(2,1)S(1)}, u32[]{:S(2)}, u32[]{:S(2)}) collective-permute-start(bf16[1,144,256]{2,1,0:T(8,128)(2,1)S(1)} %bitcast.24), channel_id=1, source_target_pairs={{0,4},{4,8},{8,12},{12,16},{16,20},{20,24},{24,28},{28,0},{1,5},{5... | collective-permute-start | bytes 221192 | tf_op jit(solution)/shard_map/ppermute | solution.py:29
  67.5 22.2 %collective-permute-done.1 = bf16[1,144,256]{2,1,0:T(8,128)(2,1)S(1)} collective-permute-done((bf16[1,144,256]{2,1,0:T(8,128)(2,1)S(1)}, bf16[1,144,256]{2,1,0:T(8,128)(2,1)S(1)}, u32[]{:S(2)}, u32[]{:S(2)}) %collective-permute-start.1) | collective-permute-done | bytes 73760 | tf_op jit(solution)/shard_map/ppermute | solution.py:29
  90.8 5.3 %collective-permute-start.2 = (bf16[3,144,256]{2,1,0:T(8,128)(2,1)S(1)}, bf16[3,144,256]{2,1,0:T(8,128)(2,1)S(1)}, u32[]{:S(2)}, u32[]{:S(2)}) collective-permute-start(bf16[3,144,256]{2,1,0:T(8,128)(2,1)S(1)} %pad_maximum_fusion.near_ref), channel_id=1, source_target_pairs={{0,12},{4,16},{8,20},{12,24},{16,28},{20,0},{24,4},{28,8},{1,13},{... | collective-permute-start | bytes 663560 | tf_op jit(solution)/shard_map/ppermute | solution.py:29
  96.1 3.6 %collective-permute-start.3 = (bf16[2,144,256]{2,1,0:T(8,128)(2,1)S(1)}, bf16[2,144,256]{2,1,0:T(8,128)(2,1)S(1)}, u32[]{:S(2)}, u32[]{:S(2)}) collective-permute-start(bf16[2,144,256]{2,1,0:T(8,128)(2,1)S(1)} %pad_maximum_fusion.1), channel_id=1, source_target_pairs={{0,20},{4,24},{8,28},{12,0},{16,4},{20,8},{24,12},{28,16},{1,21},{... | collective-permute-start | bytes 442376 | tf_op jit(solution)/shard_map/ppermute | solution.py:29
  99.7 10.0 %collective-permute-done.3.right_ref = bf16[2,144,256]{2,1,0:T(8,128)(2,1)S(1)} collective-permute-done((bf16[2,144,256]{2,1,0:T(8,128)(2,1)S(1)}, bf16[2,144,256]{2,1,0:T(8,128)(2,1)S(1)}, u32[]{:S(2)}, u32[]{:S(2)}) %collective-permute-start.3) | collective-permute-done | bytes 147488 | tf_op jit(solution)/shard_map/ppermute | solution.py:29
  111.2 2.6 %collective-permute-start.4 = (bf16[8,144,256]{2,1,0:T(8,128)(2,1)}, bf16[8,144,256]{2,1,0:T(8,128)(2,1)}, u32[]{:S(2)}, u32[]{:S(2)}) collective-permute-start(bf16[8,144,256]{2,1,0:T(8,128)(2,1)} %shard_map.79.refs_0_), channel_id=1, source_target_pairs={{0,2},{2,0},{1,3},{3,1},{4,6},{6,4},{5,7},{7,5},{8,10},{10,8},{9,1... | collective-permute-start | bytes 1769480 | tf_op jit(solution)/shard_map/ppermute | solution.py:311
  115.0 15.1 %collective-permute-done.4.refs_1_ = bf16[8,144,256]{2,1,0:T(8,128)(2,1)} collective-permute-done((bf16[8,144,256]{2,1,0:T(8,128)(2,1)}, bf16[8,144,256]{2,1,0:T(8,128)(2,1)}, u32[]{:S(2)}, u32[]{:S(2)}) %collective-permute-start.4) | collective-permute-done | bytes 589856 | tf_op jit(solution)/shard_map/ppermute | solution.py:311
  130.1 7.0 %shard_map.80 = (f32[2,16,144,128]{3,2,1,0:T(8,128)}, f32[136,256]{1,0:T(8,128)S(1)}, f32[136,256]{1,0:T(8,128)S(1)}) custom-call(s32[3]{0:T(128)S(1)} %pad_add_fusion.place_ref, bf16[2,16,144,128]{3,2,1,0:T(8,128)(2,1)S(1)} %get-tuple-element.18.z_ref, f32[8,128]{1,0:T(8,128)S(1)} %get-tuple-element.21.params_ref, ...), custom_call_target="tpu_custom_call" | custom-call | tf_op jit(solution)/shard_map/pallas_call | solution.py:38
  137.1 1.9 %collective-permute-start.5 = (f32[136,256]{1,0:T(8,128)S(1)}, f32[136,256]{1,0:T(8,128)S(1)}, u32[]{:S(2)}, u32[]{:S(2)}) collective-permute-start(f32[136,256]{1,0:T(8,128)S(1)} %get-tuple-element.23), channel_id=1, source_target_pairs={{0,1},{1,0},{2,3},{3,2},{4,5},{5,4},{6,7},{7,6},{8,9},{9,8},{10,11... | collective-permute-start | bytes 417800 | tf_op jit(solution)/shard_map/ppermute | solution.py:334
  140.3 2.9 %collective-permute-start.6 = (f32[136,128]{1,0:T(8,128)S(1)}, f32[136,128]{1,0:T(8,128)S(1)}, u32[]{:S(2)}, u32[]{:S(2)}) collective-permute-start(f32[136,128]{1,0:T(8,128)S(1)} %constant_dynamic-slice_fusion), channel_id=1, source_target_pairs={{0,32},{32,0},{1,33},{33,1},{2,34},{34,2},{3,35},{35,3},{4,36},{36... | collective-permute-start | bytes 208904 | tf_op jit(solution)/shard_map/ppermute | solution.py:338
  143.3 3.3 %collective-permute-done.6 = f32[136,128]{1,0:T(8,128)S(1)} collective-permute-done((f32[136,128]{1,0:T(8,128)S(1)}, f32[136,128]{1,0:T(8,128)S(1)}, u32[]{:S(2)}, u32[]{:S(2)}) %collective-permute-start.6) | collective-permute-done | bytes 69664 | tf_op jit(solution)/shard_map/ppermute | solution.py:338
  146.6 11.1 %all_to_all.25.got_ref = f32[8,24,128]{2,1,0:T(8,128)S(1)} all-to-all(f32[8,24,128]{2,1,0:T(8,128)S(1)} %pad_maximum_fusion.2), channel_id=1, replica_groups=mesh['z'=8,'xl'=2,'y'=8,'xh'=2,'core'=2] {'z'}, dimensions={0} | all-to-all | bytes 196608 | tf_op jit(solution)/shard_map/all_to_all | solution.py:24
  157.8 5.2 %shard_map.82 = f32[32,24,128]{2,1,0:T(8,128)} custom-call(bf16[16,144,128]{2,1,0:T(8,128)(2,1)S(1)} %all-to-all-done.held_ref, bf16[2,16,144,128]{3,2,1,0:T(8,128)(2,1)S(1)} %get-tuple-element.18.z_ref, f32[8,128]{1,0:T(8,128)S(1)} %get-tuple-element.21.params_ref, f32[2,16,144,128]{3,2,1,0:T(8,128)} %get-tuple-element.25.dxhat_ref, ...), custom_call_target="tpu_custom_call" | custom-call | tf_op jit(solution)/shard_map/pallas_call | solution.py:38
  163.0 4.5 %all-to-all-start.4 = ((f32[32,24,128]{2,1,0:T(8,128)}), f32[32,24,128]{2,1,0:T(8,128)S(1)}, u32[]{:S(2)}, u32[]{:S(2)}) async-start(f32[32,24,128]{2,1,0:T(8,128)} %shard_map.82), calls=%async_computation.4 | async-start | bytes 786432 | tf_op jit(solution)/shard_map/all_to_all | solution.py:24
  167.5 3.0 %shard_map.81 = bf16[144,256]{1,0:T(8,128)(2,1)} custom-call(bf16[16,144,256]{2,1,0:T(8,128)(2,1)S(1)} %all-to-all-done.2.whole_ref, bf16[2048,512]{1,0:T(8,128)(2,1)} %maps_ref.1), custom_call_target="tpu_custom_call" | custom-call | tf_op jit(solution)/shard_map/pallas_call | solution.py:38
  170.5 12.0 %all-to-all-done.4.got_ref = f32[32,24,128]{2,1,0:T(8,128)S(1)} async-done(((f32[32,24,128]{2,1,0:T(8,128)}), f32[32,24,128]{2,1,0:T(8,128)S(1)}, u32[]{:S(2)}, u32[]{:S(2)}) %all-to-all-start.4) | async-done | bytes 393248 | tf_op jit(solution)/shard_map/all_to_all | solution.py:24
  (29 shorter events, 8.2 us)
Async XLA Ops:
  0.6 44.2 %copy-start = (f32[2,2048]{1,0:T(2,128)S(1)}, f32[2,2048]{1,0:T(2,128)}, u32[]{:S(2)}) copy-start(f32[2,2048]{1,0:T(2,128)} %param.8) | copy-start | bytes 49156
  2.6 27.6 %all-to-all-start = ((bf16[16,144,128]{2,1,0:T(8,128)(2,1)}), bf16[16,144,128]{2,1,0:T(8,128)(2,1)S(1)}, u32[]{:S(2)}, u32[]{:S(2)}) async-start(bf16[16,144,128]{2,1,0:T(8,128)(2,1)} %shard_map.76), calls=%async_computation | async-start | bytes 1179648 | tf_op jit(solution)/shard_map/all_to_all | solution.py:24
  13.4 47.4 %copy-start.1 = (bf16[1,2,72,256]{3,2,1,0:T(8,128)(2,1)S(1)}, bf16[1,2,72,256]{3,2,1,0:T(8,128)(2,1)}, u32[]{:S(2)}) copy-start(bf16[1,2,72,256]{3,2,1,0:T(8,128)(2,1)} %param.9) | copy-start | bytes 221188
  32.9 19.8 %all-to-all-start.1 = ((f32[32,4,128]{2,1,0:T(4,128)}), f32[32,4,128]{2,1,0:T(4,128)S(1)}, u32[]{:S(2)}, u32[]{:S(2)}) async-start(f32[32,4,128]{2,1,0:T(4,128)} %get-tuple-element.19), calls=%async_computation.1 | async-start | bytes 131072 | tf_op jit(solution)/shard_map/all_to_all | solution.py:24
  54.3 92.3 %all-to-all-start.2 = ((bf16[16,144,256]{2,1,0:T(8,128)(2,1)}), bf16[16,144,256]{2,1,0:T(8,128)(2,1)S(1)}, u32[]{:S(2)}, u32[]{:S(2)}) async-start(bf16[16,144,256]{2,1,0:T(8,128)(2,1)} %get-tuple-element.20), calls=%async_computation.2 | async-start | bytes 2359296 | tf_op jit(solution)/shard_map/all_to_all | solution.py:24
  60.9 28.8 %collective-permute-start.1 = (bf16[1,144,256]{2,1,0:T(8,128)(2,1)S(1)}, bf16[1,144,256]{2,1,0:T(8,128)(2,1)S(1)}, u32[]{:S(2)}, u32[]{:S(2)}) collective-permute-start(bf16[1,144,256]{2,1,0:T(8,128)(2,1)S(1)} %bitcast.23), channel_id=1, source_target_pairs={{0,28},{4,0},{8,4},{12,8},{16,12},{20,16},{24,20},{28,24},{1,29},{... | collective-permute-start | bytes 221192 | tf_op jit(solution)/shard_map/ppermute | solution.py:29
  65.6 25.2 %collective-permute-start = (bf16[1,144,256]{2,1,0:T(8,128)(2,1)S(1)}, bf16[1,144,256]{2,1,0:T(8,128)(2,1)S(1)}, u32[]{:S(2)}, u32[]{:S(2)}) collective-permute-start(bf16[1,144,256]{2,1,0:T(8,128)(2,1)S(1)} %bitcast.24), channel_id=1, source_target_pairs={{0,4},{4,8},{8,12},{12,16},{16,20},{20,24},{24,28},{28,0},{1,5},{5... | collective-permute-start | bytes 221192 | tf_op jit(solution)/shard_map/ppermute | solution.py:29
  90.8 19.5 %collective-permute-start.2 = (bf16[3,144,256]{2,1,0:T(8,128)(2,1)S(1)}, bf16[3,144,256]{2,1,0:T(8,128)(2,1)S(1)}, u32[]{:S(2)}, u32[]{:S(2)}) collective-permute-start(bf16[3,144,256]{2,1,0:T(8,128)(2,1)S(1)} %pad_maximum_fusion.near_ref), channel_id=1, source_target_pairs={{0,12},{4,16},{8,20},{12,24},{16,28},{20,0},{24,4},{28,8},{1,13},{... | collective-permute-start | bytes 663560 | tf_op jit(solution)/shard_map/ppermute | solution.py:29
  96.1 13.6 %collective-permute-start.3 = (bf16[2,144,256]{2,1,0:T(8,128)(2,1)S(1)}, bf16[2,144,256]{2,1,0:T(8,128)(2,1)S(1)}, u32[]{:S(2)}, u32[]{:S(2)}) collective-permute-start(bf16[2,144,256]{2,1,0:T(8,128)(2,1)S(1)} %pad_maximum_fusion.1), channel_id=1, source_target_pairs={{0,20},{4,24},{8,28},{12,0},{16,4},{20,8},{24,12},{28,16},{1,21},{... | collective-permute-start | bytes 442376 | tf_op jit(solution)/shard_map/ppermute | solution.py:29
  111.2 18.9 %collective-permute-start.4 = (bf16[8,144,256]{2,1,0:T(8,128)(2,1)}, bf16[8,144,256]{2,1,0:T(8,128)(2,1)}, u32[]{:S(2)}, u32[]{:S(2)}) collective-permute-start(bf16[8,144,256]{2,1,0:T(8,128)(2,1)} %shard_map.79.refs_0_), channel_id=1, source_target_pairs={{0,2},{2,0},{1,3},{3,1},{4,6},{6,4},{5,7},{7,5},{8,10},{10,8},{9,1... | collective-permute-start | bytes 1769480 | tf_op jit(solution)/shard_map/ppermute | solution.py:311
  137.1 3.2 %collective-permute-start.5 = (f32[136,256]{1,0:T(8,128)S(1)}, f32[136,256]{1,0:T(8,128)S(1)}, u32[]{:S(2)}, u32[]{:S(2)}) collective-permute-start(f32[136,256]{1,0:T(8,128)S(1)} %get-tuple-element.23), channel_id=1, source_target_pairs={{0,1},{1,0},{2,3},{3,2},{4,5},{5,4},{6,7},{7,6},{8,9},{9,8},{10,11... | collective-permute-start | bytes 417800 | tf_op jit(solution)/shard_map/ppermute | solution.py:334
  140.3 6.2 %collective-permute-start.6 = (f32[136,128]{1,0:T(8,128)S(1)}, f32[136,128]{1,0:T(8,128)S(1)}, u32[]{:S(2)}, u32[]{:S(2)}) collective-permute-start(f32[136,128]{1,0:T(8,128)S(1)} %constant_dynamic-slice_fusion), channel_id=1, source_target_pairs={{0,32},{32,0},{1,33},{33,1},{2,34},{34,2},{3,35},{35,3},{4,36},{36... | collective-permute-start | bytes 208904 | tf_op jit(solution)/shard_map/ppermute | solution.py:338
  163.0 19.5 %all-to-all-start.4 = ((f32[32,24,128]{2,1,0:T(8,128)}), f32[32,24,128]{2,1,0:T(8,128)S(1)}, u32[]{:S(2)}, u32[]{:S(2)}) async-start(f32[32,24,128]{2,1,0:T(8,128)} %shard_map.82), calls=%async_computation.4 | async-start | bytes 786432 | tf_op jit(solution)/shard_map/all_to_all | solution.py:24

commit v3 on v2

--- a/solution.py
+++ b/solution.py
@@ -155,6 +155,7 @@
 def back_kernel(place_ref, z_ref, params_ref, gain_ref, *refs):
     *pair_refs, maps_ref, dxhat_ref, keep_ref, send_ref, total_ref, cots_ref = refs
     _, groups, _, block = z_ref.shape
+    outs = total_ref.shape[1]
     params = params_ref[...]
     gain = gain_ref[...]
     rows, half = groups // 2, place_ref[1]
@@ -168,13 +169,15 @@
     def step(g, carry):
         carry = list(carry)
         cot = cots_ref[g]
-        back = jnp.dot(cot, maps_ref[...], preferred_element_type=f32)
         used = []
         for k in range(2):
             xhat = (z_ref[k, g].astype(f32) - params[2 * k : 2 * k + 1]) * params[2 * k + 1 : 2 * k + 2]
             scaled = gain[k : k + 1] * xhat
             used.append(jnp.maximum(scaled, 0.0).astype(bf16))
-            dxhat = jnp.where(scaled > 0, back[:, k * block : (k + 1) * block], 0.0) * gain[k : k + 1]
+            back = lax.dot_general(
+                cot, maps_ref[:, k * outs : (k + 1) * outs], (((1,), (1,)), ((), ())), preferred_element_type=f32
+            )
+            dxhat = jnp.where(scaled > 0, back, 0.0) * gain[k : k + 1]
             dxhat_ref[k, g] = dxhat
             carry[2 * k] = carry[2 * k] + fold(dxhat)
             carry[2 * k + 1] = carry[2 * k + 1] + fold(dxhat * xhat)
@@ -297,7 +300,6 @@
     held, taps = lax.optimization_barrier((held, taps))
     gain = lax.dynamic_slice_in_dim(bn_gain, mine * block, block, 1)
     maps = lax.dynamic_slice_in_dim(pointwise, mine * block, block, 0)
-    maps = maps.reshape(block, 2, outs).transpose(2, 1, 0).reshape(outs, 2 * block)
 
     z, sums = call(
         functools.partial(forward_kernel, row_step),
@@ -310,6 +312,7 @@
     (column,) = call(column_kernel, [((8, pixels, outs), bf16, None)], left, near, right)
     other = lax.ppermute(column, "xh", [(0, 1), (1, 0)])
     pairs = [column, other]
+    sums, gain, maps = lax.optimization_barrier((sums, gain, maps))
     used, params = call(
         functools.partial(norm_kernel, count),
         [((groups, pixels, 2 * block), bf16, None), ((8, block), f32)],

time: 185 us -> 185 us (level)
  no operation moved by 1% of the time
where the time goes in v3:
time: 185 us; the launch traced here: 183 us
  waiting for transfers between devices  90.3 us (49%)
  starting transfers between devices  56.2 us (30%)
  Pallas kernels  22.9 us (12%)
  blocking collectives  11.1 us (6%)
    all_to_all x4, waiting for transfers between devices, exchange(): return lax.all_to_all(value, axes, 0, 0, tiled=True)  35.6 us
    ppermute x4, waiting for transfers between devices, shifted(): lax.ppermute(value, 'y', [(i, (i + steps) % count) for i in range(count)])  33.9 us
    all_to_all x4, starting transfers between devices, exchange(): return lax.all_to_all(value, axes, 0, 0, tiled=True)  33.2 us
    pallas_call x8, Pallas kernels, call(): pl.pallas_call(kernel, out_shape=[pltpu.HBM(*o[:2]) if len(o) == 3 else j...  22.9 us
    ppermute x1, waiting for transfers between devices, body(): other = lax.ppermute(column, 'xh', [(0, 1), (1, 0)])  16.2 us
    ppermute x4, starting transfers between devices, shifted(): lax.ppermute(value, 'y', [(i, (i + steps) % count) for i in range(count)])  15.4 us
    all_to_all x1, blocking collectives, exchange(): return lax.all_to_all(value, axes, 0, 0, tiled=True)  11.1 us
  transfers between devices with their start and end apart: 11, of which 10 were waited for; matrix products, arithmetic and copies ran while one was open for 1% of the time, Pallas kernels for 6%

profile of v3, /device:TPU:6, one launch (start us, length us, event | category | flops | bytes accessed | tf_op | source)
XLA Modules:
  0.0 183.1 jit_solution(17982540133682904413)
XLA Ops:
  0.6 2.0 %shard_map.76 = bf16[16,144,128]{2,1,0:T(8,128)(2,1)} custom-call(bf16[144,2048]{1,0:T(8,128)(2,1)} %bitcast.13), custom_call_target="tpu_custom_call" | custom-call | tf_op jit(solution)/shard_map/pallas_call | solution.py:38
  2.6 10.1 %all-to-all-start = ((bf16[16,144,128]{2,1,0:T(8,128)(2,1)}), bf16[16,144,128]{2,1,0:T(8,128)(2,1)S(1)}, u32[]{:S(2)}, u32[]{:S(2)}) async-start(bf16[16,144,128]{2,1,0:T(8,128)(2,1)} %shard_map.76), calls=%async_computation | async-start | bytes 1179648 | tf_op jit(solution)/shard_map/all_to_all | solution.py:24
  13.4 16.8 %all-to-all-done.held_ref = bf16[16,144,128]{2,1,0:T(8,128)(2,1)S(1)} async-done(((bf16[16,144,128]{2,1,0:T(8,128)(2,1)}), bf16[16,144,128]{2,1,0:T(8,128)(2,1)S(1)}, u32[]{:S(2)}, u32[]{:S(2)}) %all-to-all-start) | async-done | bytes 589856 | tf_op jit(solution)/shard_map/all_to_all | solution.py:24
  30.2 2.7 %shard_map.77 = (bf16[2,16,144,128]{3,2,1,0:T(8,128)(2,1)S(1)}, f32[32,4,128]{2,1,0:T(4,128)}) custom-call(bf16[16,144,128]{2,1,0:T(8,128)(2,1)S(1)} %all-to-all-done.held_ref, f32[18,128]{1,0:T(8,128)S(1)} %reshape.35.taps_ref), custom_call_target="tpu_custom_call" | custom-call | tf_op jit(solution)/shard_map/pallas_call | solution.py:38
  32.9 12.1 %all-to-all-start.1 = ((f32[32,4,128]{2,1,0:T(4,128)}), f32[32,4,128]{2,1,0:T(4,128)S(1)}, u32[]{:S(2)}, u32[]{:S(2)}) async-start(f32[32,4,128]{2,1,0:T(4,128)} %get-tuple-element.22), calls=%async_computation.1 | async-start | bytes 131072 | tf_op jit(solution)/shard_map/all_to_all | solution.py:24
  45.9 6.9 %all-to-all-done.1.sums_ref = f32[32,4,128]{2,1,0:T(4,128)S(1)} async-done(((f32[32,4,128]{2,1,0:T(4,128)}), f32[32,4,128]{2,1,0:T(4,128)S(1)}, u32[]{:S(2)}, u32[]{:S(2)}) %all-to-all-start.1) | async-done | bytes 65568 | tf_op jit(solution)/shard_map/all_to_all | solution.py:24
  54.5 6.5 %all-to-all-start.2 = ((bf16[16,144,256]{2,1,0:T(8,128)(2,1)}), bf16[16,144,256]{2,1,0:T(8,128)(2,1)S(1)}, u32[]{:S(2)}, u32[]{:S(2)}) async-start(bf16[16,144,256]{2,1,0:T(8,128)(2,1)} %get-tuple-element.25), calls=%async_computation.2 | async-start | bytes 2359296 | tf_op jit(solution)/shard_map/all_to_all | solution.py:24
  61.0 4.7 %collective-permute-start.1 = (bf16[1,144,256]{2,1,0:T(8,128)(2,1)S(1)}, bf16[1,144,256]{2,1,0:T(8,128)(2,1)S(1)}, u32[]{:S(2)}, u32[]{:S(2)}) collective-permute-start(bf16[1,144,256]{2,1,0:T(8,128)(2,1)S(1)} %bitcast.14), channel_id=1, source_target_pairs={{0,28},{4,0},{8,4},{12,8},{16,12},{20,16},{24,20},{28,24},{1,29},{... | collective-permute-start | bytes 221192 | tf_op jit(solution)/shard_map/ppermute | solution.py:29
  65.7 1.9 %collective-permute-start = (bf16[1,144,256]{2,1,0:T(8,128)(2,1)S(1)}, bf16[1,144,256]{2,1,0:T(8,128)(2,1)S(1)}, u32[]{:S(2)}, u32[]{:S(2)}) collective-permute-start(bf16[1,144,256]{2,1,0:T(8,128)(2,1)S(1)} %bitcast.15), channel_id=1, source_target_pairs={{0,4},{4,8},{8,12},{12,16},{16,20},{20,24},{24,28},{28,0},{1,5},{5... | collective-permute-start | bytes 221192 | tf_op jit(solution)/shard_map/ppermute | solution.py:29
  67.6 22.2 %collective-permute-done.1 = bf16[1,144,256]{2,1,0:T(8,128)(2,1)S(1)} collective-permute-done((bf16[1,144,256]{2,1,0:T(8,128)(2,1)S(1)}, bf16[1,144,256]{2,1,0:T(8,128)(2,1)S(1)}, u32[]{:S(2)}, u32[]{:S(2)}) %collective-permute-start.1) | collective-permute-done | bytes 73760 | tf_op jit(solution)/shard_map/ppermute | solution.py:29
  91.0 5.3 %collective-permute-start.2 = (bf16[3,144,256]{2,1,0:T(8,128)(2,1)S(1)}, bf16[3,144,256]{2,1,0:T(8,128)(2,1)S(1)}, u32[]{:S(2)}, u32[]{:S(2)}) collective-permute-start(bf16[3,144,256]{2,1,0:T(8,128)(2,1)S(1)} %pad_maximum_fusion.near_ref), channel_id=1, source_target_pairs={{0,12},{4,16},{8,20},{12,24},{16,28},{20,0},{24,4},{28,8},{1,13},{... | collective-permute-start | bytes 663560 | tf_op jit(solution)/shard_map/ppermute | solution.py:29
  96.2 3.6 %collective-permute-start.3 = (bf16[2,144,256]{2,1,0:T(8,128)(2,1)S(1)}, bf16[2,144,256]{2,1,0:T(8,128)(2,1)S(1)}, u32[]{:S(2)}, u32[]{:S(2)}) collective-permute-start(bf16[2,144,256]{2,1,0:T(8,128)(2,1)S(1)} %pad_maximum_fusion.1), channel_id=1, source_target_pairs={{0,20},{4,24},{8,28},{12,0},{16,4},{20,8},{24,12},{28,16},{1,21},{... | collective-permute-start | bytes 442376 | tf_op jit(solution)/shard_map/ppermute | solution.py:29
  99.8 10.0 %collective-permute-done.3.right_ref = bf16[2,144,256]{2,1,0:T(8,128)(2,1)S(1)} collective-permute-done((bf16[2,144,256]{2,1,0:T(8,128)(2,1)S(1)}, bf16[2,144,256]{2,1,0:T(8,128)(2,1)S(1)}, u32[]{:S(2)}, u32[]{:S(2)}) %collective-permute-start.3) | collective-permute-done | bytes 147488 | tf_op jit(solution)/shard_map/ppermute | solution.py:29
  111.3 2.6 %collective-permute-start.4 = (bf16[8,144,256]{2,1,0:T(8,128)(2,1)}, bf16[8,144,256]{2,1,0:T(8,128)(2,1)}, u32[]{:S(2)}, u32[]{:S(2)}) collective-permute-start(bf16[8,144,256]{2,1,0:T(8,128)(2,1)} %shard_map.79.refs_0_), channel_id=1, source_target_pairs={{0,2},{2,0},{1,3},{3,1},{4,6},{6,4},{5,7},{7,5},{8,10},{10,8},{9,1... | collective-permute-start | bytes 1769480 | tf_op jit(solution)/shard_map/ppermute | solution.py:313
  114.0 16.2 %collective-permute-done.4.refs_1_ = bf16[8,144,256]{2,1,0:T(8,128)(2,1)} collective-permute-done((bf16[8,144,256]{2,1,0:T(8,128)(2,1)}, bf16[8,144,256]{2,1,0:T(8,128)(2,1)}, u32[]{:S(2)}, u32[]{:S(2)}) %collective-permute-start.4) | collective-permute-done | bytes 589856 | tf_op jit(solution)/shard_map/ppermute | solution.py:313
  130.2 6.8 %shard_map.80 = (f32[2,16,144,128]{3,2,1,0:T(8,128)}, f32[136,256]{1,0:T(8,128)S(1)}, f32[136,256]{1,0:T(8,128)S(1)}) custom-call(s32[3]{0:T(128)S(1)} %pad_add_fusion.place_ref, bf16[2,16,144,128]{3,2,1,0:T(8,128)(2,1)S(1)} %get-tuple-element.21.z_ref, f32[8,128]{1,0:T(8,128)S(1)} %get-tuple-element.26.params_ref, ...), custom_call_target="tpu_custom_call" | custom-call | tf_op jit(solution)/shard_map/pallas_call | solution.py:38
  137.0 1.9 %collective-permute-start.5 = (f32[136,256]{1,0:T(8,128)S(1)}, f32[136,256]{1,0:T(8,128)S(1)}, u32[]{:S(2)}, u32[]{:S(2)}) collective-permute-start(f32[136,256]{1,0:T(8,128)S(1)} %get-tuple-element.29), channel_id=1, source_target_pairs={{0,1},{1,0},{2,3},{3,2},{4,5},{5,4},{6,7},{7,6},{8,9},{9,8},{10,11... | collective-permute-start | bytes 417800 | tf_op jit(solution)/shard_map/ppermute | solution.py:337
  140.3 2.9 %collective-permute-start.6 = (f32[136,128]{1,0:T(8,128)S(1)}, f32[136,128]{1,0:T(8,128)S(1)}, u32[]{:S(2)}, u32[]{:S(2)}) collective-permute-start(f32[136,128]{1,0:T(8,128)S(1)} %constant_dynamic-slice_fusion), channel_id=1, source_target_pairs={{0,32},{32,0},{1,33},{33,1},{2,34},{34,2},{3,35},{35,3},{4,36},{36... | collective-permute-start | bytes 208904 | tf_op jit(solution)/shard_map/ppermute | solution.py:341
  143.2 3.3 %collective-permute-done.6 = f32[136,128]{1,0:T(8,128)S(1)} collective-permute-done((f32[136,128]{1,0:T(8,128)S(1)}, f32[136,128]{1,0:T(8,128)S(1)}, u32[]{:S(2)}, u32[]{:S(2)}) %collective-permute-start.6) | collective-permute-done | bytes 69664 | tf_op jit(solution)/shard_map/ppermute | solution.py:341
  146.6 11.1 %all_to_all.25.got_ref = f32[8,24,128]{2,1,0:T(8,128)S(1)} all-to-all(f32[8,24,128]{2,1,0:T(8,128)S(1)} %pad_maximum_fusion.2), channel_id=1, replica_groups=mesh['z'=8,'xl'=2,'y'=8,'xh'=2,'core'=2] {'z'}, dimensions={0} | all-to-all | bytes 196608 | tf_op jit(solution)/shard_map/all_to_all | solution.py:24
  157.7 5.2 %shard_map.82 = f32[32,24,128]{2,1,0:T(8,128)} custom-call(bf16[16,144,128]{2,1,0:T(8,128)(2,1)S(1)} %all-to-all-done.held_ref, bf16[2,16,144,128]{3,2,1,0:T(8,128)(2,1)S(1)} %get-tuple-element.21.z_ref, f32[8,128]{1,0:T(8,128)S(1)} %get-tuple-element.26.params_ref, f32[2,16,144,128]{3,2,1,0:T(8,128)} %get-tuple-element.31.dxhat_ref, ...), custom_call_target="tpu_custom_call" | custom-call | tf_op jit(solution)/shard_map/pallas_call | solution.py:38
  162.9 4.6 %all-to-all-start.4 = ((f32[32,24,128]{2,1,0:T(8,128)}), f32[32,24,128]{2,1,0:T(8,128)S(1)}, u32[]{:S(2)}, u32[]{:S(2)}) async-start(f32[32,24,128]{2,1,0:T(8,128)} %shard_map.82), calls=%async_computation.4 | async-start | bytes 786432 | tf_op jit(solution)/shard_map/all_to_all | solution.py:24
  167.5 3.0 %shard_map.81 = bf16[144,256]{1,0:T(8,128)(2,1)} custom-call(bf16[16,144,256]{2,1,0:T(8,128)(2,1)S(1)} %all-to-all-done.2.whole_ref, bf16[2048,512]{1,0:T(8,128)(2,1)} %maps_ref.1), custom_call_target="tpu_custom_call" | custom-call | tf_op jit(solution)/shard_map/pallas_call | solution.py:38
  170.4 12.0 %all-to-all-done.4.got_ref = f32[32,24,128]{2,1,0:T(8,128)S(1)} async-done(((f32[32,24,128]{2,1,0:T(8,128)}), f32[32,24,128]{2,1,0:T(8,128)S(1)}, u32[]{:S(2)}, u32[]{:S(2)}) %all-to-all-start.4) | async-done | bytes 393248 | tf_op jit(solution)/shard_map/all_to_all | solution.py:24
  (27 shorter events, 8.1 us)
Async XLA Ops:
  0.6 44.4 %copy-start = (f32[2,2048]{1,0:T(2,128)S(1)}, f32[2,2048]{1,0:T(2,128)}, u32[]{:S(2)}) copy-start(f32[2,2048]{1,0:T(2,128)} %param.8) | copy-start | bytes 49156
  2.6 27.6 %all-to-all-start = ((bf16[16,144,128]{2,1,0:T(8,128)(2,1)}), bf16[16,144,128]{2,1,0:T(8,128)(2,1)S(1)}, u32[]{:S(2)}, u32[]{:S(2)}) async-start(bf16[16,144,128]{2,1,0:T(8,128)(2,1)} %shard_map.76), calls=%async_computation | async-start | bytes 1179648 | tf_op jit(solution)/shard_map/all_to_all | solution.py:24
  32.9 28.1 %copy-start.1 = (bf16[1,2,72,256]{3,2,1,0:T(8,128)(2,1)S(1)}, bf16[1,2,72,256]{3,2,1,0:T(8,128)(2,1)}, u32[]{:S(2)}) copy-start(bf16[1,2,72,256]{3,2,1,0:T(8,128)(2,1)} %param.9) | copy-start | bytes 221188
  32.9 19.9 %all-to-all-start.1 = ((f32[32,4,128]{2,1,0:T(4,128)}), f32[32,4,128]{2,1,0:T(4,128)S(1)}, u32[]{:S(2)}, u32[]{:S(2)}) async-start(f32[32,4,128]{2,1,0:T(4,128)} %get-tuple-element.22), calls=%async_computation.1 | async-start | bytes 131072 | tf_op jit(solution)/shard_map/all_to_all | solution.py:24
  54.5 92.1 %all-to-all-start.2 = ((bf16[16,144,256]{2,1,0:T(8,128)(2,1)}), bf16[16,144,256]{2,1,0:T(8,128)(2,1)S(1)}, u32[]{:S(2)}, u32[]{:S(2)}) async-start(bf16[16,144,256]{2,1,0:T(8,128)(2,1)} %get-tuple-element.25), calls=%async_computation.2 | async-start | bytes 2359296 | tf_op jit(solution)/shard_map/all_to_all | solution.py:24
  61.0 28.8 %collective-permute-start.1 = (bf16[1,144,256]{2,1,0:T(8,128)(2,1)S(1)}, bf16[1,144,256]{2,1,0:T(8,128)(2,1)S(1)}, u32[]{:S(2)}, u32[]{:S(2)}) collective-permute-start(bf16[1,144,256]{2,1,0:T(8,128)(2,1)S(1)} %bitcast.14), channel_id=1, source_target_pairs={{0,28},{4,0},{8,4},{12,8},{16,12},{20,16},{24,20},{28,24},{1,29},{... | collective-permute-start | bytes 221192 | tf_op jit(solution)/shard_map/ppermute | solution.py:29
  65.7 25.2 %collective-permute-start = (bf16[1,144,256]{2,1,0:T(8,128)(2,1)S(1)}, bf16[1,144,256]{2,1,0:T(8,128)(2,1)S(1)}, u32[]{:S(2)}, u32[]{:S(2)}) collective-permute-start(bf16[1,144,256]{2,1,0:T(8,128)(2,1)S(1)} %bitcast.15), channel_id=1, source_target_pairs={{0,4},{4,8},{8,12},{12,16},{16,20},{20,24},{24,28},{28,0},{1,5},{5... | collective-permute-start | bytes 221192 | tf_op jit(solution)/shard_map/ppermute | solution.py:29
  91.0 19.5 %collective-permute-start.2 = (bf16[3,144,256]{2,1,0:T(8,128)(2,1)S(1)}, bf16[3,144,256]{2,1,0:T(8,128)(2,1)S(1)}, u32[]{:S(2)}, u32[]{:S(2)}) collective-permute-start(bf16[3,144,256]{2,1,0:T(8,128)(2,1)S(1)} %pad_maximum_fusion.near_ref), channel_id=1, source_target_pairs={{0,12},{4,16},{8,20},{12,24},{16,28},{20,0},{24,4},{28,8},{1,13},{... | collective-permute-start | bytes 663560 | tf_op jit(solution)/shard_map/ppermute | solution.py:29
  96.2 13.6 %collective-permute-start.3 = (bf16[2,144,256]{2,1,0:T(8,128)(2,1)S(1)}, bf16[2,144,256]{2,1,0:T(8,128)(2,1)S(1)}, u32[]{:S(2)}, u32[]{:S(2)}) collective-permute-start(bf16[2,144,256]{2,1,0:T(8,128)(2,1)S(1)} %pad_maximum_fusion.1), channel_id=1, source_target_pairs={{0,20},{4,24},{8,28},{12,0},{16,4},{20,8},{24,12},{28,16},{1,21},{... | collective-permute-start | bytes 442376 | tf_op jit(solution)/shard_map/ppermute | solution.py:29
  111.3 18.9 %collective-permute-start.4 = (bf16[8,144,256]{2,1,0:T(8,128)(2,1)}, bf16[8,144,256]{2,1,0:T(8,128)(2,1)}, u32[]{:S(2)}, u32[]{:S(2)}) collective-permute-start(bf16[8,144,256]{2,1,0:T(8,128)(2,1)} %shard_map.79.refs_0_), channel_id=1, source_target_pairs={{0,2},{2,0},{1,3},{3,1},{4,6},{6,4},{5,7},{7,5},{8,10},{10,8},{9,1... | collective-permute-start | bytes 1769480 | tf_op jit(solution)/shard_map/ppermute | solution.py:313
  137.0 3.2 %collective-permute-start.5 = (f32[136,256]{1,0:T(8,128)S(1)}, f32[136,256]{1,0:T(8,128)S(1)}, u32[]{:S(2)}, u32[]{:S(2)}) collective-permute-start(f32[136,256]{1,0:T(8,128)S(1)} %get-tuple-element.29), channel_id=1, source_target_pairs={{0,1},{1,0},{2,3},{3,2},{4,5},{5,4},{6,7},{7,6},{8,9},{9,8},{10,11... | collective-permute-start | bytes 417800 | tf_op jit(solution)/shard_map/ppermute | solution.py:337
  140.3 6.2 %collective-permute-start.6 = (f32[136,128]{1,0:T(8,128)S(1)}, f32[136,128]{1,0:T(8,128)S(1)}, u32[]{:S(2)}, u32[]{:S(2)}) collective-permute-start(f32[136,128]{1,0:T(8,128)S(1)} %constant_dynamic-slice_fusion), channel_id=1, source_target_pairs={{0,32},{32,0},{1,33},{33,1},{2,34},{34,2},{3,35},{35,3},{4,36},{36... | collective-permute-start | bytes 208904 | tf_op jit(solution)/shard_map/ppermute | solution.py:341
  162.9 19.5 %all-to-all-start.4 = ((f32[32,24,128]{2,1,0:T(8,128)}), f32[32,24,128]{2,1,0:T(8,128)S(1)}, u32[]{:S(2)}, u32[]{:S(2)}) async-start(f32[32,24,128]{2,1,0:T(8,128)} %shard_map.82), calls=%async_computation.4 | async-start | bytes 786432 | tf_op jit(solution)/shard_map/all_to_all | solution.py:24

commit v4 on v3

--- a/solution.py
+++ b/solution.py
@@ -238,8 +238,10 @@
         jnp.where(low, pltpu.roll(tiles[0], share, 1), tiles[1]),
     )
     for i in range(out_ref.shape[0]):
-        out_ref[i, :lines, :] = got[i % 2 * lines : (i % 2 + 1) * lines]
-        out_ref[i, lines:, :] = halves[i % 2]
+        rows_sent = [got[i % 2 * lines + 4 * j : i % 2 * lines + 4 * (j + 1)] for j in range(lines // 4)]
+        rows_sent += [halves[i % 2][4 * j : 4 * (j + 1)] for j in range(3)]
+        for j, value in enumerate(rows_sent):
+            out_ref[i, j] = value
 
 
 def mix_kernel(whole_ref, maps_ref, out_ref):
@@ -258,17 +260,22 @@
 
 
 def last_kernel(got_ref, pw_ref, dw_ref):
-    peers, total, block = got_ref.shape
+    peers, tiles, four, block = got_ref.shape
     share, wide = pw_ref.shape
-    lines = total - 16
+    tiles -= 3
+    lines = tiles * four
     lanes = wide // 2 // block
     for i in range(peers):
         k, lane, row = place_of(i)
         left = (k * lanes + lane) * block
-        pw_ref[row * lines : (row + 1) * lines, left : left + block] = got_ref[i, :lines, :]
-    dw = jnp.sum(got_ref[:, lines:, :], axis=0)
-    dw_ref[:, 0, :] = dw[:9, :share]
-    dw_ref[:, 1, :] = pltpu.roll(dw, share, 1)[:9, :share]
+        for j in range(tiles):
+            top = row * lines + j * four
+            pw_ref[top : top + four, left : left + block] = got_ref[i, j]
+    dw = jnp.sum(got_ref[:, tiles:], axis=0)
+    for t in range(9):
+        line = dw[t // four, t % four : t % four + 1]
+        dw_ref[t, 0:1, :] = line[:, :share]
+        dw_ref[t, 1:2, :] = pltpu.roll(line, share, 1)[:, :share]
 
 
 def body(features, depthwise, pointwise, bn_gain, cotangent):
@@ -288,7 +295,7 @@
     pad = pltpu.VMEM((groups + 2 * lead, row_count, width + 2 * FAR_DILATION, block), f32)
     lines = share * 2 * outs // peers // block
 
-    (sent,) = call(pack_kernel, [((groups, pixels, block), bf16, None)], features.reshape(pixels, channels), slow=(0,))
+    (sent,) = call(pack_kernel, [((groups, pixels, block), bf16)], features.reshape(pixels, channels), slow=(0,))
     held = exchange(sent, GROUP)
     cot = cotangent.reshape(1, pixels, outs)
     above = shifted(cot, 1)
@@ -303,7 +310,7 @@
 
     z, sums = call(
         functools.partial(forward_kernel, row_step),
-        [((2, groups, pixels, block), bf16), ((peers, 4, block), f32, None)],
+        [((2, groups, pixels, block), bf16), ((peers, 4, block), f32)],
         held,
         taps,
         scratch=[pad],
@@ -314,11 +321,7 @@
     pairs = [column, other]
     sums, gain, maps = lax.optimization_barrier((sums, gain, maps))
     used, params = call(
-        functools.partial(norm_kernel, count),
-        [((groups, pixels, 2 * block), bf16, None), ((8, block), f32)],
-        z,
-        sums,
-        gain,
+        functools.partial(norm_kernel, count), [((groups, pixels, 2 * block), bf16), ((8, block), f32)], z, sums, gain
     )
     whole = exchange(used, GROUP)
     dxhat, keep, sent = call(
@@ -346,7 +349,7 @@
     got = exchange(sent, "z")
     (sent,) = call(
         functools.partial(filter_kernel, row_step, count),
-        [((peers, lines + 16, block), f32, None)],
+        [((peers, lines // 4 + 3, 4, block), f32)],
         held,
         z,
         params,

time: 185 us -> 183 us (0.989)
  no operation moved by 1% of the time
where the time goes in v4:
time: 183 us; the launch traced here: 182 us
  waiting for transfers between devices  88.9 us (49%)
  starting transfers between devices  56.2 us (31%)
  Pallas kernels  21.8 us (12%)
  blocking collectives  11.1 us (6%)
  local copies, waits for them, and re-layouts  2.03 us (1%)
    all_to_all x4, waiting for transfers between devices, exchange(): return lax.all_to_all(value, axes, 0, 0, tiled=True)  34.2 us
    ppermute x4, waiting for transfers between devices, shifted(): lax.ppermute(value, 'y', [(i, (i + steps) % count) for i in range(count)])  33.9 us
    all_to_all x4, starting transfers between devices, exchange(): return lax.all_to_all(value, axes, 0, 0, tiled=True)  33.2 us
    pallas_call x8, Pallas kernels, call(): pl.pallas_call(kernel, out_shape=[pltpu.HBM(*o[:2]) if len(o) == 3 else j...  21.8 us
    ppermute x1, waiting for transfers between devices, body(): other = lax.ppermute(column, 'xh', [(0, 1), (1, 0)])  16.2 us
    ppermute x4, starting transfers between devices, shifted(): lax.ppermute(value, 'y', [(i, (i + steps) % count) for i in range(count)])  15.4 us
    all_to_all x1, blocking collectives, exchange(): return lax.all_to_all(value, axes, 0, 0, tiled=True)  11.1 us
  transfers between devices with their start and end apart: 11, of which 10 were waited for; matrix products, arithmetic and copies ran while one was open for 1% of the time, Pallas kernels for 6%

profile of v4, /device:TPU:6, one launch (start us, length us, event | category | flops | bytes accessed | tf_op | source)
XLA Modules:
  0.0 181.7 jit_solution(12143991556410798239)
XLA Ops:
  0.6 2.0 %shard_map.76 = bf16[16,144,128]{2,1,0:T(8,128)(2,1)} custom-call(bf16[144,2048]{1,0:T(8,128)(2,1)} %bitcast.13), custom_call_target="tpu_custom_call" | custom-call | tf_op jit(solution)/shard_map/pallas_call | solution.py:38
  2.6 10.1 %all-to-all-start = ((bf16[16,144,128]{2,1,0:T(8,128)(2,1)}), bf16[16,144,128]{2,1,0:T(8,128)(2,1)S(1)}, u32[]{:S(2)}, u32[]{:S(2)}) async-start(bf16[16,144,128]{2,1,0:T(8,128)(2,1)} %shard_map.76), calls=%async_computation | async-start | bytes 1179648 | tf_op jit(solution)/shard_map/all_to_all | solution.py:24
  13.4 16.8 %all-to-all-done.held_ref = bf16[16,144,128]{2,1,0:T(8,128)(2,1)S(1)} async-done(((bf16[16,144,128]{2,1,0:T(8,128)(2,1)}), bf16[16,144,128]{2,1,0:T(8,128)(2,1)S(1)}, u32[]{:S(2)}, u32[]{:S(2)}) %all-to-all-start) | async-done | bytes 589856 | tf_op jit(solution)/shard_map/all_to_all | solution.py:24
  30.2 2.7 %shard_map.77 = (bf16[2,16,144,128]{3,2,1,0:T(8,128)(2,1)S(1)}, f32[32,4,128]{2,1,0:T(4,128)}) custom-call(bf16[16,144,128]{2,1,0:T(8,128)(2,1)S(1)} %all-to-all-done.held_ref, f32[18,128]{1,0:T(8,128)S(1)} %reshape.35.taps_ref), custom_call_target="tpu_custom_call" | custom-call | tf_op jit(solution)/shard_map/pallas_call | solution.py:38
  32.9 12.1 %all-to-all-start.1 = ((f32[32,4,128]{2,1,0:T(4,128)}), f32[32,4,128]{2,1,0:T(4,128)S(1)}, u32[]{:S(2)}, u32[]{:S(2)}) async-start(f32[32,4,128]{2,1,0:T(4,128)} %get-tuple-element.22), calls=%async_computation.1 | async-start | bytes 131072 | tf_op jit(solution)/shard_map/all_to_all | solution.py:24
  45.9 6.9 %all-to-all-done.1.sums_ref = f32[32,4,128]{2,1,0:T(4,128)S(1)} async-done(((f32[32,4,128]{2,1,0:T(4,128)}), f32[32,4,128]{2,1,0:T(4,128)S(1)}, u32[]{:S(2)}, u32[]{:S(2)}) %all-to-all-start.1) | async-done | bytes 65568 | tf_op jit(solution)/shard_map/all_to_all | solution.py:24
  54.5 6.5 %all-to-all-start.2 = ((bf16[16,144,256]{2,1,0:T(8,128)(2,1)}), bf16[16,144,256]{2,1,0:T(8,128)(2,1)S(1)}, u32[]{:S(2)}, u32[]{:S(2)}) async-start(bf16[16,144,256]{2,1,0:T(8,128)(2,1)} %copy-done.1), calls=%async_computation.2 | async-start | bytes 2359296 | tf_op jit(solution)/shard_map/all_to_all | solution.py:24
  61.0 4.7 %collective-permute-start.1 = (bf16[1,144,256]{2,1,0:T(8,128)(2,1)S(1)}, bf16[1,144,256]{2,1,0:T(8,128)(2,1)S(1)}, u32[]{:S(2)}, u32[]{:S(2)}) collective-permute-start(bf16[1,144,256]{2,1,0:T(8,128)(2,1)S(1)} %bitcast.14), channel_id=1, source_target_pairs={{0,28},{4,0},{8,4},{12,8},{16,12},{20,16},{24,20},{28,24},{1,29},{... | collective-permute-start | bytes 221192 | tf_op jit(solution)/shard_map/ppermute | solution.py:29
  65.7 1.9 %collective-permute-start = (bf16[1,144,256]{2,1,0:T(8,128)(2,1)S(1)}, bf16[1,144,256]{2,1,0:T(8,128)(2,1)S(1)}, u32[]{:S(2)}, u32[]{:S(2)}) collective-permute-start(bf16[1,144,256]{2,1,0:T(8,128)(2,1)S(1)} %bitcast.15), channel_id=1, source_target_pairs={{0,4},{4,8},{8,12},{12,16},{16,20},{20,24},{24,28},{28,0},{1,5},{5... | collective-permute-start | bytes 221192 | tf_op jit(solution)/shard_map/ppermute | solution.py:29
  67.6 22.2 %collective-permute-done.1 = bf16[1,144,256]{2,1,0:T(8,128)(2,1)S(1)} collective-permute-done((bf16[1,144,256]{2,1,0:T(8,128)(2,1)S(1)}, bf16[1,144,256]{2,1,0:T(8,128)(2,1)S(1)}, u32[]{:S(2)}, u32[]{:S(2)}) %collective-permute-start.1) | collective-permute-done | bytes 73760 | tf_op jit(solution)/shard_map/ppermute | solution.py:29
  91.0 5.3 %collective-permute-start.2 = (bf16[3,144,256]{2,1,0:T(8,128)(2,1)S(1)}, bf16[3,144,256]{2,1,0:T(8,128)(2,1)S(1)}, u32[]{:S(2)}, u32[]{:S(2)}) collective-permute-start(bf16[3,144,256]{2,1,0:T(8,128)(2,1)S(1)} %pad_maximum_fusion.near_ref), channel_id=1, source_target_pairs={{0,12},{4,16},{8,20},{12,24},{16,28},{20,0},{24,4},{28,8},{1,13},{... | collective-permute-start | bytes 663560 | tf_op jit(solution)/shard_map/ppermute | solution.py:29
  96.2 3.6 %collective-permute-start.3 = (bf16[2,144,256]{2,1,0:T(8,128)(2,1)S(1)}, bf16[2,144,256]{2,1,0:T(8,128)(2,1)S(1)}, u32[]{:S(2)}, u32[]{:S(2)}) collective-permute-start(bf16[2,144,256]{2,1,0:T(8,128)(2,1)S(1)} %pad_maximum_fusion.1), channel_id=1, source_target_pairs={{0,20},{4,24},{8,28},{12,0},{16,4},{20,8},{24,12},{28,16},{1,21},{... | collective-permute-start | bytes 442376 | tf_op jit(solution)/shard_map/ppermute | solution.py:29
  99.8 10.0 %collective-permute-done.3.right_ref = bf16[2,144,256]{2,1,0:T(8,128)(2,1)S(1)} collective-permute-done((bf16[2,144,256]{2,1,0:T(8,128)(2,1)S(1)}, bf16[2,144,256]{2,1,0:T(8,128)(2,1)S(1)}, u32[]{:S(2)}, u32[]{:S(2)}) %collective-permute-start.3) | collective-permute-done | bytes 147488 | tf_op jit(solution)/shard_map/ppermute | solution.py:29
  111.3 2.6 %collective-permute-start.4 = (bf16[8,144,256]{2,1,0:T(8,128)(2,1)}, bf16[8,144,256]{2,1,0:T(8,128)(2,1)}, u32[]{:S(2)}, u32[]{:S(2)}) collective-permute-start(bf16[8,144,256]{2,1,0:T(8,128)(2,1)} %shard_map.79.refs_0_), channel_id=1, source_target_pairs={{0,2},{2,0},{1,3},{3,1},{4,6},{6,4},{5,7},{7,5},{8,10},{10,8},{9,1... | collective-permute-start | bytes 1769480 | tf_op jit(solution)/shard_map/ppermute | solution.py:320
  114.0 16.2 %collective-permute-done.4.refs_1_ = bf16[8,144,256]{2,1,0:T(8,128)(2,1)} collective-permute-done((bf16[8,144,256]{2,1,0:T(8,128)(2,1)}, bf16[8,144,256]{2,1,0:T(8,128)(2,1)}, u32[]{:S(2)}, u32[]{:S(2)}) %collective-permute-start.4) | collective-permute-done | bytes 589856 | tf_op jit(solution)/shard_map/ppermute | solution.py:320
  130.2 6.8 %shard_map.80 = (f32[2,16,144,128]{3,2,1,0:T(8,128)}, f32[136,256]{1,0:T(8,128)S(1)}, f32[136,256]{1,0:T(8,128)S(1)}) custom-call(s32[3]{0:T(128)S(1)} %pad_add_fusion.place_ref, bf16[2,16,144,128]{3,2,1,0:T(8,128)(2,1)S(1)} %get-tuple-element.21.z_ref, f32[8,128]{1,0:T(8,128)S(1)} %get-tuple-element.26.params_ref, ...), custom_call_target="tpu_custom_call" | custom-call | tf_op jit(solution)/shard_map/pallas_call | solution.py:38
  137.0 1.9 %collective-permute-start.5 = (f32[136,256]{1,0:T(8,128)S(1)}, f32[136,256]{1,0:T(8,128)S(1)}, u32[]{:S(2)}, u32[]{:S(2)}) collective-permute-start(f32[136,256]{1,0:T(8,128)S(1)} %get-tuple-element.29), channel_id=1, source_target_pairs={{0,1},{1,0},{2,3},{3,2},{4,5},{5,4},{6,7},{7,6},{8,9},{9,8},{10,11... | collective-permute-start | bytes 417800 | tf_op jit(solution)/shard_map/ppermute | solution.py:340
  140.3 2.9 %collective-permute-start.6 = (f32[136,128]{1,0:T(8,128)S(1)}, f32[136,128]{1,0:T(8,128)S(1)}, u32[]{:S(2)}, u32[]{:S(2)}) collective-permute-start(f32[136,128]{1,0:T(8,128)S(1)} %constant_dynamic-slice_fusion), channel_id=1, source_target_pairs={{0,32},{32,0},{1,33},{33,1},{2,34},{34,2},{3,35},{35,3},{4,36},{36... | collective-permute-start | bytes 208904 | tf_op jit(solution)/shard_map/ppermute | solution.py:344
  143.2 3.3 %collective-permute-done.6 = f32[136,128]{1,0:T(8,128)S(1)} collective-permute-done((f32[136,128]{1,0:T(8,128)S(1)}, f32[136,128]{1,0:T(8,128)S(1)}, u32[]{:S(2)}, u32[]{:S(2)}) %collective-permute-start.6) | collective-permute-done | bytes 69664 | tf_op jit(solution)/shard_map/ppermute | solution.py:344
  146.6 11.1 %all_to_all.25.got_ref = f32[8,24,128]{2,1,0:T(8,128)S(1)} all-to-all(f32[8,24,128]{2,1,0:T(8,128)S(1)} %pad_maximum_fusion.2), channel_id=1, replica_groups=mesh['z'=8,'xl'=2,'y'=8,'xh'=2,'core'=2] {'z'}, dimensions={0} | all-to-all | bytes 196608 | tf_op jit(solution)/shard_map/all_to_all | solution.py:24
  157.7 5.2 %shard_map.82 = f32[32,5,4,128]{3,2,1,0:T(4,128)} custom-call(bf16[16,144,128]{2,1,0:T(8,128)(2,1)S(1)} %all-to-all-done.held_ref, bf16[2,16,144,128]{3,2,1,0:T(8,128)(2,1)S(1)} %get-tuple-element.21.z_ref, f32[8,128]{1,0:T(8,128)S(1)} %get-tuple-element.26.params_ref, f32[2,16,144,128]{3,2,1,0:T(8,128)} %get-tuple-element.31.dxhat_ref, ...), custom_call_target="tpu_custom_call" | custom-call | tf_op jit(solution)/shard_map/pallas_call | solution.py:38
  162.9 4.5 %all-to-all-start.4 = ((f32[32,5,4,128]{3,2,1,0:T(4,128)}), f32[32,5,4,128]{3,2,1,0:T(4,128)S(1)}, u32[]{:S(2)}, u32[]{:S(2)}) async-start(f32[32,5,4,128]{3,2,1,0:T(4,128)} %shard_map.82), calls=%async_computation.4 | async-start | bytes 655360 | tf_op jit(solution)/shard_map/all_to_all | solution.py:24
  167.4 3.0 %shard_map.81 = bf16[144,256]{1,0:T(8,128)(2,1)} custom-call(bf16[16,144,256]{2,1,0:T(8,128)(2,1)S(1)} %all-to-all-done.2.whole_ref, bf16[2048,512]{1,0:T(8,128)(2,1)} %maps_ref.1), custom_call_target="tpu_custom_call" | custom-call | tf_op jit(solution)/shard_map/pallas_call | solution.py:38
  170.4 10.6 %all-to-all-done.4.got_ref = f32[32,5,4,128]{3,2,1,0:T(4,128)S(1)} async-done(((f32[32,5,4,128]{3,2,1,0:T(4,128)}), f32[32,5,4,128]{3,2,1,0:T(4,128)S(1)}, u32[]{:S(2)}, u32[]{:S(2)}) %all-to-all-start.4) | async-done | bytes 327712 | tf_op jit(solution)/shard_map/all_to_all | solution.py:24
  (29 shorter events, 8.1 us)
Async XLA Ops:
  0.6 44.3 %copy-start = (f32[2,2048]{1,0:T(2,128)S(1)}, f32[2,2048]{1,0:T(2,128)}, u32[]{:S(2)}) copy-start(f32[2,2048]{1,0:T(2,128)} %param.8) | copy-start | bytes 49156
  2.6 27.6 %all-to-all-start = ((bf16[16,144,128]{2,1,0:T(8,128)(2,1)}), bf16[16,144,128]{2,1,0:T(8,128)(2,1)S(1)}, u32[]{:S(2)}, u32[]{:S(2)}) async-start(bf16[16,144,128]{2,1,0:T(8,128)(2,1)} %shard_map.76), calls=%async_computation | async-start | bytes 1179648 | tf_op jit(solution)/shard_map/all_to_all | solution.py:24
  32.9 28.1 %copy-start.2 = (bf16[1,2,72,256]{3,2,1,0:T(8,128)(2,1)S(1)}, bf16[1,2,72,256]{3,2,1,0:T(8,128)(2,1)}, u32[]{:S(2)}) copy-start(bf16[1,2,72,256]{3,2,1,0:T(8,128)(2,1)} %param.9) | copy-start | bytes 221188
  32.9 19.9 %all-to-all-start.1 = ((f32[32,4,128]{2,1,0:T(4,128)}), f32[32,4,128]{2,1,0:T(4,128)S(1)}, u32[]{:S(2)}, u32[]{:S(2)}) async-start(f32[32,4,128]{2,1,0:T(4,128)} %get-tuple-element.22), calls=%async_computation.1 | async-start | bytes 131072 | tf_op jit(solution)/shard_map/all_to_all | solution.py:24
  53.4 1.1 copy-start.1
  54.5 92.1 %all-to-all-start.2 = ((bf16[16,144,256]{2,1,0:T(8,128)(2,1)}), bf16[16,144,256]{2,1,0:T(8,128)(2,1)S(1)}, u32[]{:S(2)}, u32[]{:S(2)}) async-start(bf16[16,144,256]{2,1,0:T(8,128)(2,1)} %copy-done.1), calls=%async_computation.2 | async-start | bytes 2359296 | tf_op jit(solution)/shard_map/all_to_all | solution.py:24
  61.0 28.8 %collective-permute-start.1 = (bf16[1,144,256]{2,1,0:T(8,128)(2,1)S(1)}, bf16[1,144,256]{2,1,0:T(8,128)(2,1)S(1)}, u32[]{:S(2)}, u32[]{:S(2)}) collective-permute-start(bf16[1,144,256]{2,1,0:T(8,128)(2,1)S(1)} %bitcast.14), channel_id=1, source_target_pairs={{0,28},{4,0},{8,4},{12,8},{16,12},{20,16},{24,20},{28,24},{1,29},{... | collective-permute-start | bytes 221192 | tf_op jit(solution)/shard_map/ppermute | solution.py:29
  65.7 25.2 %collective-permute-start = (bf16[1,144,256]{2,1,0:T(8,128)(2,1)S(1)}, bf16[1,144,256]{2,1,0:T(8,128)(2,1)S(1)}, u32[]{:S(2)}, u32[]{:S(2)}) collective-permute-start(bf16[1,144,256]{2,1,0:T(8,128)(2,1)S(1)} %bitcast.15), channel_id=1, source_target_pairs={{0,4},{4,8},{8,12},{12,16},{16,20},{20,24},{24,28},{28,0},{1,5},{5... | collective-permute-start | bytes 221192 | tf_op jit(solution)/shard_map/ppermute | solution.py:29
  91.0 19.5 %collective-permute-start.2 = (bf16[3,144,256]{2,1,0:T(8,128)(2,1)S(1)}, bf16[3,144,256]{2,1,0:T(8,128)(2,1)S(1)}, u32[]{:S(2)}, u32[]{:S(2)}) collective-permute-start(bf16[3,144,256]{2,1,0:T(8,128)(2,1)S(1)} %pad_maximum_fusion.near_ref), channel_id=1, source_target_pairs={{0,12},{4,16},{8,20},{12,24},{16,28},{20,0},{24,4},{28,8},{1,13},{... | collective-permute-start | bytes 663560 | tf_op jit(solution)/shard_map/ppermute | solution.py:29
  96.2 13.6 %collective-permute-start.3 = (bf16[2,144,256]{2,1,0:T(8,128)(2,1)S(1)}, bf16[2,144,256]{2,1,0:T(8,128)(2,1)S(1)}, u32[]{:S(2)}, u32[]{:S(2)}) collective-permute-start(bf16[2,144,256]{2,1,0:T(8,128)(2,1)S(1)} %pad_maximum_fusion.1), channel_id=1, source_target_pairs={{0,20},{4,24},{8,28},{12,0},{16,4},{20,8},{24,12},{28,16},{1,21},{... | collective-permute-start | bytes 442376 | tf_op jit(solution)/shard_map/ppermute | solution.py:29
  111.3 18.9 %collective-permute-start.4 = (bf16[8,144,256]{2,1,0:T(8,128)(2,1)}, bf16[8,144,256]{2,1,0:T(8,128)(2,1)}, u32[]{:S(2)}, u32[]{:S(2)}) collective-permute-start(bf16[8,144,256]{2,1,0:T(8,128)(2,1)} %shard_map.79.refs_0_), channel_id=1, source_target_pairs={{0,2},{2,0},{1,3},{3,1},{4,6},{6,4},{5,7},{7,5},{8,10},{10,8},{9,1... | collective-permute-start | bytes 1769480 | tf_op jit(solution)/shard_map/ppermute | solution.py:320
  137.0 3.2 %collective-permute-start.5 = (f32[136,256]{1,0:T(8,128)S(1)}, f32[136,256]{1,0:T(8,128)S(1)}, u32[]{:S(2)}, u32[]{:S(2)}) collective-permute-start(f32[136,256]{1,0:T(8,128)S(1)} %get-tuple-element.29), channel_id=1, source_target_pairs={{0,1},{1,0},{2,3},{3,2},{4,5},{5,4},{6,7},{7,6},{8,9},{9,8},{10,11... | collective-permute-start | bytes 417800 | tf_op jit(solution)/shard_map/ppermute | solution.py:340
  140.3 6.2 %collective-permute-start.6 = (f32[136,128]{1,0:T(8,128)S(1)}, f32[136,128]{1,0:T(8,128)S(1)}, u32[]{:S(2)}, u32[]{:S(2)}) collective-permute-start(f32[136,128]{1,0:T(8,128)S(1)} %constant_dynamic-slice_fusion), channel_id=1, source_target_pairs={{0,32},{32,0},{1,33},{33,1},{2,34},{34,2},{3,35},{35,3},{4,36},{36... | collective-permute-start | bytes 208904 | tf_op jit(solution)/shard_map/ppermute | solution.py:344
  162.9 18.1 %all-to-all-start.4 = ((f32[32,5,4,128]{3,2,1,0:T(4,128)}), f32[32,5,4,128]{3,2,1,0:T(4,128)S(1)}, u32[]{:S(2)}, u32[]{:S(2)}) async-start(f32[32,5,4,128]{3,2,1,0:T(4,128)} %shard_map.82), calls=%async_computation.4 | async-start | bytes 655360 | tf_op jit(solution)/shard_map/all_to_all | solution.py:24

commit v5 on v4

--- a/solution.py
+++ b/solution.py
@@ -13,7 +13,7 @@
 eps_norm = 1e-05
 
 GROUP = ("y", "xh")
-ORDER = (-4, -3, -2, -1, 0, 1, 2, 3)
+ORDER = (-2, 0, 2, 4)
 DP = ("z", "xl")
 ROWS = ("z", "xl", "core")
 f32 = jnp.float32
@@ -51,10 +51,10 @@
         out_ref[g] = feat_ref[:, g * block : (g + 1) * block]
 
 
-def column_kernel(left_ref, near_ref, right_ref, out_ref):
-    out_ref[:3] = left_ref[...]
-    out_ref[3:6] = near_ref[...]
-    out_ref[6:] = right_ref[...]
+def column_kernel(*refs):
+    *pair_refs, out_ref = refs
+    for i, ref in enumerate(pair_refs):
+        out_ref[2 * i : 2 * i + 2] = ref[...]
 
 
 def fill_padded(held_ref, pad):
@@ -164,7 +164,8 @@
     for slot, ref in enumerate(pair_refs):
         for i, apart in enumerate(ORDER):
             row = (place_ref[0] + apart + rows) % rows
-            cots_ref[2 * row + (half ^ slot)] = ref[i]
+            for j in range(2):
+                cots_ref[2 * (row ^ j) + (half ^ slot)] = ref[2 * i + j]
 
     def step(g, carry):
         carry = list(carry)
@@ -298,16 +299,17 @@
     (sent,) = call(pack_kernel, [((groups, pixels, block), bf16)], features.reshape(pixels, channels), slow=(0,))
     held = exchange(sent, GROUP)
     cot = cotangent.reshape(1, pixels, outs)
-    above = shifted(cot, 1)
-    below = shifted(cot, -1)
-    near = jnp.concatenate([above, cot, below], axis=0)
-    left = shifted(near, 3)
-    right = shifted(near[:2], -3)
+    count_y = lax.axis_size("y")
+    beside = lax.ppermute(cot, "y", [(i, i ^ 1) for i in range(count_y)])
+    near = jnp.concatenate([cot, beside], axis=0)
+    left = shifted(near, 2)
+    right = shifted(near, -2)
+    far = shifted(near, 4)
     taps = lax.dynamic_slice_in_dim(depthwise, mine * block, block, 2).astype(f32).reshape(18, block)
-    held, taps = lax.optimization_barrier((held, taps))
     gain = lax.dynamic_slice_in_dim(bn_gain, mine * block, block, 1)
     maps = lax.dynamic_slice_in_dim(pointwise, mine * block, block, 0)
 
+    held, taps, gain, maps = lax.optimization_barrier((held, taps, gain, maps))
     z, sums = call(
         functools.partial(forward_kernel, row_step),
         [((2, groups, pixels, block), bf16), ((peers, 4, block), f32)],
@@ -316,10 +318,9 @@
         scratch=[pad],
     )
     sums = exchange(sums, ROWS)
-    (column,) = call(column_kernel, [((8, pixels, outs), bf16, None)], left, near, right)
+    (column,) = call(column_kernel, [((8, pixels, outs), bf16, None)], left, near, right, far)
     other = lax.ppermute(column, "xh", [(0, 1), (1, 0)])
     pairs = [column, other]
-    sums, gain, maps = lax.optimization_barrier((sums, gain, maps))
     used, params = call(
         functools.partial(norm_kernel, count), [((groups, pixels, 2 * block), bf16), ((8, block), f32)], z, sums, gain
     )

time: 183 us -> 185 us (1.011); the launches traced: 182 us -> 182 us
  blocking collectives: 11.1 us -> 30.7 us
  starting transfers between devices: 56.2 us -> 46.4 us
  waiting for transfers between devices: 88.9 us -> 79.6 us
    ppermute x4 -> x3, waiting for transfers between devices: 33.9 us -> 7.93 us  [shifted(): lax.ppermute(value, 'y', [(i, (i + steps) % count) for i in range(count)])]
    ppermute x0 -> x1, waiting for transfers between devices: none -> 25.4 us  [body(): beside = lax.ppermute(cot, 'y', [(i, i ^ 1) for i in range(count_y)])]
    all_to_all x1 -> x2, blocking collectives: 11.1 us -> 30.7 us  [exchange(): return lax.all_to_all(value, axes, 0, 0, tiled=True)]
    all_to_all x4 -> x3, starting transfers between devices: 33.2 us -> 21.2 us  [exchange(): return lax.all_to_all(value, axes, 0, 0, tiled=True)]
    all_to_all x4 -> x3, waiting for transfers between devices: 34.2 us -> 26.4 us  [exchange(): return lax.all_to_all(value, axes, 0, 0, tiled=True)]
    ppermute x0 -> x1, starting transfers between devices: none -> 3.38 us  [body(): beside = lax.ppermute(cot, 'y', [(i, i ^ 1) for i in range(count_y)])]
    ppermute x4 -> x3, starting transfers between devices: 15.4 us -> 14.3 us  [shifted(): lax.ppermute(value, 'y', [(i, (i + steps) % count) for i in range(count)])]
  transfers between devices with their start and end apart: 11 -> 10, of which waited for: 10 -> 7; matrix products, arithmetic and copies ran while one was open for 1% -> 1% of each run, Pallas kernels for 6% -> 6%
where the time goes in v5:
time: 185 us; the launch traced here: 182 us
  waiting for transfers between devices  79.6 us (43%)
  starting transfers between devices  46.4 us (25%)
  blocking collectives  30.7 us (17%)
  Pallas kernels  21.2 us (11%)
  local copies, waits for them, and re-layouts  2.03 us (1%)
    all_to_all x2, blocking collectives, exchange(): return lax.all_to_all(value, axes, 0, 0, tiled=True)  30.7 us
    all_to_all x3, waiting for transfers between devices, exchange(): return lax.all_to_all(value, axes, 0, 0, tiled=True)  26.4 us
    ppermute x1, waiting for transfers between devices, body(): beside = lax.ppermute(cot, 'y', [(i, i ^ 1) for i in range(count_y)])  25.4 us
    all_to_all x3, starting transfers between devices, exchange(): return lax.all_to_all(value, axes, 0, 0, tiled=True)  21.2 us
    pallas_call x8, Pallas kernels, call(): pl.pallas_call(kernel, out_shape=[pltpu.HBM(*o[:2]) if len(o) == 3 else j...  21.2 us
    ppermute x1, waiting for transfers between devices, body(): other = lax.ppermute(column, 'xh', [(0, 1), (1, 0)])  15.4 us
    ppermute x3, starting transfers between devices, shifted(): lax.ppermute(value, 'y', [(i, (i + steps) % count) for i in range(count)])  14.3 us
    ppermute x3, waiting for transfers between devices, shifted(): lax.ppermute(value, 'y', [(i, (i + steps) % count) for i in range(count)])  7.93 us
  transfers between devices with their start and end apart: 10, of which 7 were waited for; matrix products, arithmetic and copies ran while one was open for 1% of the time, Pallas kernels for 6%

profile of v5, /device:TPU:6, one launch (start us, length us, event | category | flops | bytes accessed | tf_op | source)
XLA Modules:
  0.0 181.5 jit_solution(17370295736770232931)
XLA Ops:
  0.6 2.0 %shard_map.76 = bf16[16,144,128]{2,1,0:T(8,128)(2,1)} custom-call(bf16[144,2048]{1,0:T(8,128)(2,1)} %bitcast.13), custom_call_target="tpu_custom_call" | custom-call | tf_op jit(solution)/shard_map/pallas_call | solution.py:38
  2.6 10.1 %all-to-all-start = ((bf16[16,144,128]{2,1,0:T(8,128)(2,1)}), bf16[16,144,128]{2,1,0:T(8,128)(2,1)S(1)}, u32[]{:S(2)}, u32[]{:S(2)}) async-start(bf16[16,144,128]{2,1,0:T(8,128)(2,1)} %shard_map.76), calls=%async_computation | async-start | bytes 1179648 | tf_op jit(solution)/shard_map/all_to_all | solution.py:24
  14.4 15.8 %all-to-all-done.held_ref = bf16[16,144,128]{2,1,0:T(8,128)(2,1)S(1)} async-done(((bf16[16,144,128]{2,1,0:T(8,128)(2,1)}), bf16[16,144,128]{2,1,0:T(8,128)(2,1)S(1)}, u32[]{:S(2)}, u32[]{:S(2)}) %all-to-all-start) | async-done | bytes 589856 | tf_op jit(solution)/shard_map/all_to_all | solution.py:24
  30.2 2.1 %shard_map.77 = (bf16[2,16,144,128]{3,2,1,0:T(8,128)(2,1)S(1)}, f32[32,4,128]{2,1,0:T(4,128)S(1)}) custom-call(bf16[16,144,128]{2,1,0:T(8,128)(2,1)S(1)} %all-to-all-done.held_ref, f32[18,128]{1,0:T(8,128)S(1)} %reshape.35.taps_ref), custom_call_target="tpu_custom_call" | custom-call | tf_op jit(solution)/shard_map/pallas_call | solution.py:38
  32.3 19.6 %all_to_all.25.sums_ref = f32[32,4,128]{2,1,0:T(4,128)S(1)} all-to-all(f32[32,4,128]{2,1,0:T(4,128)S(1)} %get-tuple-element.21), channel_id=1, replica_groups=mesh['z'=8,'xl'=2,'y'=8,'xh'=2,'core'=2] {'z','xl','core'}, dimensions={0} | all-to-all | bytes 131072 | tf_op jit(solution)/shard_map/all_to_all | solution.py:24
  53.5 6.5 %all-to-all-start.2 = ((bf16[16,144,256]{2,1,0:T(8,128)(2,1)}), bf16[16,144,256]{2,1,0:T(8,128)(2,1)S(1)}, u32[]{:S(2)}, u32[]{:S(2)}) async-start(bf16[16,144,256]{2,1,0:T(8,128)(2,1)} %copy-done.1), calls=%async_computation.2 | async-start | bytes 2359296 | tf_op jit(solution)/shard_map/all_to_all | solution.py:24
  60.0 3.4 %collective-permute-start = (bf16[1,144,256]{2,1,0:T(8,128)(2,1)S(1)}, bf16[1,144,256]{2,1,0:T(8,128)(2,1)S(1)}, u32[]{:S(2)}, u32[]{:S(2)}) collective-permute-start(bf16[1,144,256]{2,1,0:T(8,128)(2,1)S(1)} %bitcast.17), channel_id=1, source_target_pairs={{0,4},{4,0},{8,12},{12,8},{16,20},{20,16},{24,28},{28,24},{1,5},{5... | collective-permute-start | bytes 221192 | tf_op jit(solution)/shard_map/ppermute | solution.py:303
  63.4 25.4 %collective-permute-done = bf16[1,144,256]{2,1,0:T(8,128)(2,1)S(1)} collective-permute-done((bf16[1,144,256]{2,1,0:T(8,128)(2,1)S(1)}, bf16[1,144,256]{2,1,0:T(8,128)(2,1)S(1)}, u32[]{:S(2)}, u32[]{:S(2)}) %collective-permute-start) | collective-permute-done | bytes 73760 | tf_op jit(solution)/shard_map/ppermute | solution.py:303
  88.8 4.4 %collective-permute-start.1 = (bf16[2,144,256]{2,1,0:T(8,128)(2,1)S(1)}, bf16[2,144,256]{2,1,0:T(8,128)(2,1)S(1)}, u32[]{:S(2)}, u32[]{:S(2)}) collective-permute-start(bf16[2,144,256]{2,1,0:T(8,128)(2,1)S(1)} %pad_maximum_fusion.refs_1_), channel_id=1, source_target_pairs={{0,8},{4,12},{8,16},{12,20},{16,24},{20,28},{24,0},{28,4},{1,9},{5... | collective-permute-start | bytes 442376 | tf_op jit(solution)/shard_map/ppermute | solution.py:29
  93.2 3.6 %collective-permute-start.2 = (bf16[2,144,256]{2,1,0:T(8,128)(2,1)S(1)}, bf16[2,144,256]{2,1,0:T(8,128)(2,1)S(1)}, u32[]{:S(2)}, u32[]{:S(2)}) collective-permute-start(bf16[2,144,256]{2,1,0:T(8,128)(2,1)S(1)} %pad_maximum_fusion.refs_1_), channel_id=1, source_target_pairs={{0,24},{4,28},{8,0},{12,4},{16,8},{20,12},{24,16},{28,20},{1,25},{... | collective-permute-start | bytes 442376 | tf_op jit(solution)/shard_map/ppermute | solution.py:29
  96.8 6.4 %collective-permute-start.3 = (bf16[2,144,256]{2,1,0:T(8,128)(2,1)S(1)}, bf16[2,144,256]{2,1,0:T(8,128)(2,1)S(1)}, u32[]{:S(2)}, u32[]{:S(2)}) collective-permute-start(bf16[2,144,256]{2,1,0:T(8,128)(2,1)S(1)} %pad_maximum_fusion.refs_1_), channel_id=1, source_target_pairs={{0,16},{4,20},{8,24},{12,28},{16,0},{20,4},{24,8},{28,12},{1,17},{... | collective-permute-start | bytes 442376 | tf_op jit(solution)/shard_map/ppermute | solution.py:29
  103.3 7.9 %collective-permute-done.3.refs_3_ = bf16[2,144,256]{2,1,0:T(8,128)(2,1)S(1)} collective-permute-done((bf16[2,144,256]{2,1,0:T(8,128)(2,1)S(1)}, bf16[2,144,256]{2,1,0:T(8,128)(2,1)S(1)}, u32[]{:S(2)}, u32[]{:S(2)}) %collective-permute-start.3) | collective-permute-done | bytes 147488 | tf_op jit(solution)/shard_map/ppermute | solution.py:29
  112.0 2.6 %collective-permute-start.4 = (bf16[8,144,256]{2,1,0:T(8,128)(2,1)}, bf16[8,144,256]{2,1,0:T(8,128)(2,1)}, u32[]{:S(2)}, u32[]{:S(2)}) collective-permute-start(bf16[8,144,256]{2,1,0:T(8,128)(2,1)} %shard_map.79.refs_0_), channel_id=1, source_target_pairs={{0,2},{2,0},{1,3},{3,1},{4,6},{6,4},{5,7},{7,5},{8,10},{10,8},{9,1... | collective-permute-start | bytes 1769480 | tf_op jit(solution)/shard_map/ppermute | solution.py:322
  114.7 15.4 %collective-permute-done.4.refs_1_ = bf16[8,144,256]{2,1,0:T(8,128)(2,1)} collective-permute-done((bf16[8,144,256]{2,1,0:T(8,128)(2,1)}, bf16[8,144,256]{2,1,0:T(8,128)(2,1)}, u32[]{:S(2)}, u32[]{:S(2)}) %collective-permute-start.4) | collective-permute-done | bytes 589856 | tf_op jit(solution)/shard_map/ppermute | solution.py:322
  130.0 6.8 %shard_map.80 = (f32[2,16,144,128]{3,2,1,0:T(8,128)}, f32[136,256]{1,0:T(8,128)S(1)}, f32[136,256]{1,0:T(8,128)S(1)}) custom-call(s32[3]{0:T(128)S(1)} %pad_add_fusion.place_ref, bf16[2,16,144,128]{3,2,1,0:T(8,128)(2,1)S(1)} %get-tuple-element.20.z_ref, f32[8,128]{1,0:T(8,128)S(1)} %get-tuple-element.24.params_ref, ...), custom_call_target="tpu_custom_call" | custom-call | tf_op jit(solution)/shard_map/pallas_call | solution.py:38
  136.8 1.9 %collective-permute-start.5 = (f32[136,256]{1,0:T(8,128)S(1)}, f32[136,256]{1,0:T(8,128)S(1)}, u32[]{:S(2)}, u32[]{:S(2)}) collective-permute-start(f32[136,256]{1,0:T(8,128)S(1)} %get-tuple-element.27), channel_id=1, source_target_pairs={{0,1},{1,0},{2,3},{3,2},{4,5},{5,4},{6,7},{7,6},{8,9},{9,8},{10,11... | collective-permute-start | bytes 417800 | tf_op jit(solution)/shard_map/ppermute | solution.py:341
  138.7 1.3 collective-permute-done.5
  140.1 3.0 %collective-permute-start.6 = (f32[136,128]{1,0:T(8,128)S(1)}, f32[136,128]{1,0:T(8,128)S(1)}, u32[]{:S(2)}, u32[]{:S(2)}) collective-permute-start(f32[136,128]{1,0:T(8,128)S(1)} %constant_dynamic-slice_fusion), channel_id=1, source_target_pairs={{0,32},{32,0},{1,33},{33,1},{2,34},{34,2},{3,35},{35,3},{4,36},{36... | collective-permute-start | bytes 208904 | tf_op jit(solution)/shard_map/ppermute | solution.py:345
  143.1 3.2 %collective-permute-done.6 = f32[136,128]{1,0:T(8,128)S(1)} collective-permute-done((f32[136,128]{1,0:T(8,128)S(1)}, f32[136,128]{1,0:T(8,128)S(1)}, u32[]{:S(2)}, u32[]{:S(2)}) %collective-permute-start.6) | collective-permute-done | bytes 69664 | tf_op jit(solution)/shard_map/ppermute | solution.py:345
  146.4 11.2 %all_to_all.26.got_ref = f32[8,24,128]{2,1,0:T(8,128)S(1)} all-to-all(f32[8,24,128]{2,1,0:T(8,128)S(1)} %pad_maximum_fusion.1), channel_id=1, replica_groups=mesh['z'=8,'xl'=2,'y'=8,'xh'=2,'core'=2] {'z'}, dimensions={0} | all-to-all | bytes 196608 | tf_op jit(solution)/shard_map/all_to_all | solution.py:24
  157.5 5.2 %shard_map.82 = f32[32,5,4,128]{3,2,1,0:T(4,128)} custom-call(bf16[16,144,128]{2,1,0:T(8,128)(2,1)S(1)} %all-to-all-done.held_ref, bf16[2,16,144,128]{3,2,1,0:T(8,128)(2,1)S(1)} %get-tuple-element.20.z_ref, f32[8,128]{1,0:T(8,128)S(1)} %get-tuple-element.24.params_ref, f32[2,16,144,128]{3,2,1,0:T(8,128)} %get-tuple-element.29.dxhat_ref, ...), custom_call_target="tpu_custom_call" | custom-call | tf_op jit(solution)/shard_map/pallas_call | solution.py:38
  162.7 4.6 %all-to-all-start.4 = ((f32[32,5,4,128]{3,2,1,0:T(4,128)}), f32[32,5,4,128]{3,2,1,0:T(4,128)S(1)}, u32[]{:S(2)}, u32[]{:S(2)}) async-start(f32[32,5,4,128]{3,2,1,0:T(4,128)} %shard_map.82), calls=%async_computation.4 | async-start | bytes 655360 | tf_op jit(solution)/shard_map/all_to_all | solution.py:24
  167.3 3.0 %shard_map.81 = bf16[144,256]{1,0:T(8,128)(2,1)} custom-call(bf16[16,144,256]{2,1,0:T(8,128)(2,1)S(1)} %all-to-all-done.2.whole_ref, bf16[2048,512]{1,0:T(8,128)(2,1)} %maps_ref.1), custom_call_target="tpu_custom_call" | custom-call | tf_op jit(solution)/shard_map/pallas_call | solution.py:38
  170.2 10.6 %all-to-all-done.4.got_ref = f32[32,5,4,128]{3,2,1,0:T(4,128)S(1)} async-done(((f32[32,5,4,128]{3,2,1,0:T(4,128)}), f32[32,5,4,128]{3,2,1,0:T(4,128)S(1)}, u32[]{:S(2)}, u32[]{:S(2)}) %all-to-all-start.4) | async-done | bytes 327712 | tf_op jit(solution)/shard_map/all_to_all | solution.py:24
  (27 shorter events, 5.1 us)
Async XLA Ops:
  0.6 12.8 %copy-start = (f32[2,2048]{1,0:T(2,128)S(1)}, f32[2,2048]{1,0:T(2,128)}, u32[]{:S(2)}) copy-start(f32[2,2048]{1,0:T(2,128)} %param.8) | copy-start | bytes 49156
  2.6 27.6 %all-to-all-start = ((bf16[16,144,128]{2,1,0:T(8,128)(2,1)}), bf16[16,144,128]{2,1,0:T(8,128)(2,1)S(1)}, u32[]{:S(2)}, u32[]{:S(2)}) async-start(bf16[16,144,128]{2,1,0:T(8,128)(2,1)} %shard_map.76), calls=%async_computation | async-start | bytes 1179648 | tf_op jit(solution)/shard_map/all_to_all | solution.py:24
  14.4 45.7 %copy-start.2 = (bf16[1,2,72,256]{3,2,1,0:T(8,128)(2,1)S(1)}, bf16[1,2,72,256]{3,2,1,0:T(8,128)(2,1)}, u32[]{:S(2)}) copy-start(bf16[1,2,72,256]{3,2,1,0:T(8,128)(2,1)} %param.9) | copy-start | bytes 221188
  52.4 1.0 copy-start.1
  53.5 92.9 %all-to-all-start.2 = ((bf16[16,144,256]{2,1,0:T(8,128)(2,1)}), bf16[16,144,256]{2,1,0:T(8,128)(2,1)S(1)}, u32[]{:S(2)}, u32[]{:S(2)}) async-start(bf16[16,144,256]{2,1,0:T(8,128)(2,1)} %copy-done.1), calls=%async_computation.2 | async-start | bytes 2359296 | tf_op jit(solution)/shard_map/all_to_all | solution.py:24
  60.0 28.8 %collective-permute-start = (bf16[1,144,256]{2,1,0:T(8,128)(2,1)S(1)}, bf16[1,144,256]{2,1,0:T(8,128)(2,1)S(1)}, u32[]{:S(2)}, u32[]{:S(2)}) collective-permute-start(bf16[1,144,256]{2,1,0:T(8,128)(2,1)S(1)} %bitcast.17), channel_id=1, source_target_pairs={{0,4},{4,0},{8,12},{12,8},{16,20},{20,16},{24,28},{28,24},{1,5},{5... | collective-permute-start | bytes 221192 | tf_op jit(solution)/shard_map/ppermute | solution.py:303
  88.8 14.4 %collective-permute-start.1 = (bf16[2,144,256]{2,1,0:T(8,128)(2,1)S(1)}, bf16[2,144,256]{2,1,0:T(8,128)(2,1)S(1)}, u32[]{:S(2)}, u32[]{:S(2)}) collective-permute-start(bf16[2,144,256]{2,1,0:T(8,128)(2,1)S(1)} %pad_maximum_fusion.refs_1_), channel_id=1, source_target_pairs={{0,8},{4,12},{8,16},{12,20},{16,24},{20,28},{24,0},{28,4},{1,9},{5... | collective-permute-start | bytes 442376 | tf_op jit(solution)/shard_map/ppermute | solution.py:29
  93.2 10.0 %collective-permute-start.2 = (bf16[2,144,256]{2,1,0:T(8,128)(2,1)S(1)}, bf16[2,144,256]{2,1,0:T(8,128)(2,1)S(1)}, u32[]{:S(2)}, u32[]{:S(2)}) collective-permute-start(bf16[2,144,256]{2,1,0:T(8,128)(2,1)S(1)} %pad_maximum_fusion.refs_1_), channel_id=1, source_target_pairs={{0,24},{4,28},{8,0},{12,4},{16,8},{20,12},{24,16},{28,20},{1,25},{... | collective-permute-start | bytes 442376 | tf_op jit(solution)/shard_map/ppermute | solution.py:29
  96.8 14.3 %collective-permute-start.3 = (bf16[2,144,256]{2,1,0:T(8,128)(2,1)S(1)}, bf16[2,144,256]{2,1,0:T(8,128)(2,1)S(1)}, u32[]{:S(2)}, u32[]{:S(2)}) collective-permute-start(bf16[2,144,256]{2,1,0:T(8,128)(2,1)S(1)} %pad_maximum_fusion.refs_1_), channel_id=1, source_target_pairs={{0,16},{4,20},{8,24},{12,28},{16,0},{20,4},{24,8},{28,12},{1,17},{... | collective-permute-start | bytes 442376 | tf_op jit(solution)/shard_map/ppermute | solution.py:29
  112.0 18.0 %collective-permute-start.4 = (bf16[8,144,256]{2,1,0:T(8,128)(2,1)}, bf16[8,144,256]{2,1,0:T(8,128)(2,1)}, u32[]{:S(2)}, u32[]{:S(2)}) collective-permute-start(bf16[8,144,256]{2,1,0:T(8,128)(2,1)} %shard_map.79.refs_0_), channel_id=1, source_target_pairs={{0,2},{2,0},{1,3},{3,1},{4,6},{6,4},{5,7},{7,5},{8,10},{10,8},{9,1... | collective-permute-start | bytes 1769480 | tf_op jit(solution)/shard_map/ppermute | solution.py:322
  136.8 3.2 %collective-permute-start.5 = (f32[136,256]{1,0:T(8,128)S(1)}, f32[136,256]{1,0:T(8,128)S(1)}, u32[]{:S(2)}, u32[]{:S(2)}) collective-permute-start(f32[136,256]{1,0:T(8,128)S(1)} %get-tuple-element.27), channel_id=1, source_target_pairs={{0,1},{1,0},{2,3},{3,2},{4,5},{5,4},{6,7},{7,6},{8,9},{9,8},{10,11... | collective-permute-start | bytes 417800 | tf_op jit(solution)/shard_map/ppermute | solution.py:341
  140.1 6.2 %collective-permute-start.6 = (f32[136,128]{1,0:T(8,128)S(1)}, f32[136,128]{1,0:T(8,128)S(1)}, u32[]{:S(2)}, u32[]{:S(2)}) collective-permute-start(f32[136,128]{1,0:T(8,128)S(1)} %constant_dynamic-slice_fusion), channel_id=1, source_target_pairs={{0,32},{32,0},{1,33},{33,1},{2,34},{34,2},{3,35},{35,3},{4,36},{36... | collective-permute-start | bytes 208904 | tf_op jit(solution)/shard_map/ppermute | solution.py:345
  162.7 18.1 %all-to-all-start.4 = ((f32[32,5,4,128]{3,2,1,0:T(4,128)}), f32[32,5,4,128]{3,2,1,0:T(4,128)S(1)}, u32[]{:S(2)}, u32[]{:S(2)}) async-start(f32[32,5,4,128]{3,2,1,0:T(4,128)} %shard_map.82), calls=%async_computation.4 | async-start | bytes 655360 | tf_op jit(solution)/shard_map/all_to_all | solution.py:24
